TPU v7x, 32 devices: a whole 2x2x4 slice. The times are simulated.
32 devices in a mesh: occ: 4 (over y, x), vir: 8 (over z, core).
Axes of the slice: x: 2, y: 2, z: 4, core: 2. Of those that a mesh axis runs over, the one named last changes fastest.
Arguments:
- amplitudes: bfloat16 [1504, 3072], P('occ', 'vir'), may hold values from -6 to 6
- integrals: bfloat16 [3072, 3072], P(None, 'vir'), may hold values from -0.15625 to 0.15625
- tile_block: int32 [24], replicated, may hold values from 0 to 5, as said below
- pair_mask: int32 [6, 6], replicated, may hold values 0 or 1
- partner: int32 [1504], P('occ'), may hold values from 0 to 1503, as said below
Outputs:
- residual: float32 [1504, 3072], P('occ', 'vir')
Inputs may be any that keep to these rules, and one draw needn't show every extreme that they name: partner is an involution without fixed points: partner[partner[r]] = r and partner[r] != r. tile_block never falls along the tiles, and each of the 6 blocks holds at least one tile.
All inputs are finite; a program needn't handle non-finite values.
Results may differ from a plain program's by a relative error of at most 0.0003.
Values may be sent and summed in bfloat16 or wider, within the bound.
No kernel may reach another device: no remote copies, remote signals or barrier semaphores. Data moves between devices by JAX's collectives and lax.ppermute only.
A program may use at most 128 MiB of HBM per device.

v0:
```python
import functools

import jax
import jax.numpy as jnp
from jax import lax
from jax.experimental import pallas as pl
from jax.experimental.pallas import tpu as pltpu
from jax.sharding import PartitionSpec as P

TILE = 128
SCALE = 4096.0


def split(values):
    wide = values.astype(jnp.float32)
    high = lax.reduce_precision(wide, 8, 7)
    return high.astype(jnp.bfloat16), (wide - high).astype(jnp.bfloat16)


def trade(values, distance):
    return lax.ppermute(values, "vir", [(i, i ^ distance) for i in range(8)])


def contract_kernel(count, scale, order_ref, live_ref, *refs):
    pieces, refs = refs[: 2 * count], refs[2 * count :]
    base_ref = refs[0] if len(refs) == 5 else None
    integrals_ref, out_ref, block_ref, sems = refs[-4:]
    depth = block_ref.shape[1]
    tiles = depth // TILE
    copies = []
    for i in range(count):
        start = pl.multiple_of(order_ref[i] * depth, TILE)
        copies.append(
            pltpu.make_async_copy(
                integrals_ref.at[pl.ds(start, depth), :], block_ref.at[i], sems.at[i]
            )
        )
        copies[-1].start()
    total = None
    for i in range(count):
        copies[i].wait()
        rows = []
        for t in range(tiles):
            mask = live_ref[pl.ds(order_ref[i] * tiles + t, 1), :].astype(jnp.bfloat16)
            rows.append(block_ref[i, t * TILE : (t + 1) * TILE, :] * mask)
        block = jnp.concatenate(rows, axis=0)
        for part in pieces[2 * i : 2 * i + 2]:
            term = jnp.dot(part[...], block, preferred_element_type=jnp.float32)
            total = term if total is None else total + term
    if base_ref is not None:
        total = total + base_ref[...]
    out_ref[...] = total * scale if scale != 1.0 else total


def contract_body(items, order, live, integrals, base=None, scale=1.0):
    count = len(items)
    rows, depth = items[0].shape
    columns = integrals.shape[1]
    parts = [part for item in items for part in split(item)]
    extra = [] if base is None else [base]
    vmem = pl.BlockSpec(memory_space=pltpu.VMEM)
    flops = 4 * count * rows * depth * columns
    return pl.pallas_call(
        functools.partial(contract_kernel, count, scale),
        out_shape=jax.ShapeDtypeStruct((rows, columns), jnp.float32),
        in_specs=[pl.BlockSpec(memory_space=pltpu.SMEM), vmem]
        + [vmem] * (len(parts) + len(extra))
        + [pl.BlockSpec(memory_space=pl.ANY)],
        out_specs=vmem,
        scratch_shapes=[
            pltpu.VMEM((count, depth, columns), jnp.bfloat16),
            pltpu.SemaphoreType.DMA((count,)),
        ],
        compiler_params=pltpu.CompilerParams(vmem_limit_bytes=12 << 20),
        cost_estimate=pl.CostEstimate(
            flops=flops, transcendentals=0, bytes_accessed=2 * count * depth * columns
        ),
    )(jnp.stack(order).astype(jnp.int32), live, *parts, *extra, integrals)


def body(amplitudes, integrals, tile_block, pair_mask, partner, occ, vir):
    rows, _ = amplitudes.shape
    columns = integrals.shape[1]
    local_tiles = columns // TILE
    total_tiles = tile_block.shape[0]
    groups = pair_mask.shape[0]
    here = lax.axis_index("vir")
    me = lax.axis_index("occ")

    slots = jnp.arange(rows, dtype=jnp.int32)

    def picked(block, source):
        onehot = (partner[:, None] == source * rows + slots[None, :]).astype(jnp.bfloat16)
        return jnp.dot(onehot, block, preferred_element_type=jnp.float32)

    received = [
        lax.ppermute(amplitudes, "occ", [(i, i ^ k) for i in range(occ)]) for k in range(1, occ)
    ]
    difference = amplitudes.astype(jnp.float32) - picked(amplitudes, me)
    for k in range(1, occ):
        difference = difference - picked(received[k - 1], me ^ k)
    own = (difference * SCALE).astype(jnp.float16)

    labels = jnp.arange(groups, dtype=jnp.int32)
    own_blocks = lax.dynamic_slice_in_dim(tile_block, here * local_tiles, local_tiles)
    row_onehot = (tile_block[:, None] == labels[None, :]).astype(jnp.float32)
    col_onehot = (own_blocks[:, None] == labels[None, :]).astype(jnp.float32)
    live = jnp.dot(jnp.dot(row_onehot, pair_mask.astype(jnp.float32)), col_onehot.T)
    live = jnp.repeat(live, TILE, axis=1)

    if vir != 8:
        masked = integrals.reshape(total_tiles, TILE, columns)
        masked = masked * live.astype(jnp.bfloat16)[:, None, :]
        masked = masked.reshape(integrals.shape)
        high, low = split(lax.all_gather(own, "vir", axis=1, tiled=True))
        total = jnp.dot(high, masked, preferred_element_type=jnp.float32)
        total = total + jnp.dot(low, masked, preferred_element_type=jnp.float32)
        return total * (1.0 / SCALE)

    plane, core = here // 2, here % 2

    def place(step, other):
        return (plane ^ step) * 2 + (core ^ other)

    own = lax.optimization_barrier(own)
    third = trade(own, 6)
    first = trade(own, 2)
    second = trade(third, 2)
    total = contract_body(
        [own, trade(own, 1)], [place(0, 0), place(0, 1)], live, integrals
    )
    total = contract_body(
        [first, trade(first, 1), third, trade(third, 1)],
        [place(1, 0), place(1, 1), place(3, 0), place(3, 1)],
        live,
        integrals,
        total,
    )
    total = contract_body([second], [place(2, 0)], live, integrals, total)
    return contract_body(
        [trade(second, 1)], [place(2, 1)], live, integrals, total, 1.0 / SCALE
    )


def solution(mesh):
    occ, vir = mesh.shape["occ"], mesh.shape["vir"]

    def whole(*args):
        return body(*args, occ, vir)

    placed = (P("occ", "vir"), P(None, "vir"), P(), P(), P("occ"))
    return jax.shard_map(
        whole, mesh=mesh, in_specs=placed, out_specs=P("occ", "vir"), check_vma=False
    )
```

profile of v0, /device:TPU:0, one launch (start us, length us, event | category | flops | bytes accessed | tf_op | source)
XLA Modules:
  0.0 50.9 jit_solution(1550081378077694993)
XLA Ops:
  0.0 0.0 copy-start.1
  0.0 3.9 %collective-permute-start.2 = (bf16[376,384]{1,0:T(8,128)(2,1)}, bf16[376,384]{1,0:T(8,128)(2,1)S(1)}, u32[]{:S(2)}, u32[]{:S(2)}) collective-permute-start(bf16[376,384]{1,0:T(8,128)(2,1)} %param.5), channel_id=1, source_target_pairs={{0,24},{8,16},{16,8},{24,0},{1,25},{9,17},{17,9},{25,1},{2,26},{10... | collective-permute-start | bytes 866312 | tf_op jit(solution)/shard_map/ppermute | solution.py:97
  3.9 0.5 collective-permute-start.1
  4.4 0.1 collective-permute-start
  4.6 0.7 %dynamic_slice.3 = s32[3]{0:T(128)S(1)} dynamic-slice(s32[24]{0:T(128)} %param.7, s32[]{:T(128)S(6)} %select_n.16), dynamic_slice_sizes={3} | dynamic-slice | bytes 28 | tf_op jit(solution)/shard_map/dynamic_slice | solution.py:105
  5.3 1.5 %convolution_subtract_fusion.1 = f32[376,384]{1,0:T(8,128)S(1)} fusion(bf16[376,384]{1,0:T(8,128)(2,1)} %param.5, s32[376]{0:T(512)S(1)} %iota_add_fusion.3, s32[376]{0:T(512)} %param.9), kind=kOutput, calls=%fused_computation.1 | convolution fusion | flops 109006912 | bytes 869312 | tf_op jit(solution)/shard_map/dot_general | solution.py:94
  6.8 1.0 %fusion.4 = f32[24,3]{1,0:T(8,128)S(1)} fusion(s32[24]{0:T(128)} %param.7, s32[6,6]{1,0:T(8,128)} %param.8, s32[3]{0:T(128)S(1)} %dynamic_slice.3), kind=kOutput, calls=%fused_computation.6 | convolution fusion | flops 2790 | bytes 540 | tf_op jit(solution)/shard_map/dot_general | solution.py:108
  7.8 0.1 pad_add_fusion.1.order_ref
  7.9 4.0 %collective-permute-done.2 = bf16[376,384]{1,0:T(8,128)(2,1)S(1)} collective-permute-done((bf16[376,384]{1,0:T(8,128)(2,1)}, bf16[376,384]{1,0:T(8,128)(2,1)S(1)}, u32[]{:S(2)}, u32[]{:S(2)}) %collective-permute-start.2) | collective-permute-done | bytes 288800 | tf_op jit(solution)/shard_map/ppermute | solution.py:97
  11.9 1.1 %fusion.15 = f32[376,384]{1,0:T(8,128)S(1)} fusion(bf16[376,384]{1,0:T(8,128)(2,1)S(1)} %collective-permute-done.2, s32[376]{0:T(512)S(1)} %iota_add_fusion, s32[376]{0:T(512)} %param.9), kind=kOutput, calls=%fused_computation.32 | convolution fusion | flops 108718144 | bytes 869312 | tf_op jit(solution)/shard_map/dot_general | solution.py:94
  13.0 4.2 %collective-permute-done.1 = bf16[376,384]{1,0:T(8,128)(2,1)S(1)} collective-permute-done((bf16[376,384]{1,0:T(8,128)(2,1)}, bf16[376,384]{1,0:T(8,128)(2,1)S(1)}, u32[]{:S(2)}, u32[]{:S(2)}) %collective-permute-start.1) | collective-permute-done | bytes 288800 | tf_op jit(solution)/shard_map/ppermute | solution.py:97
  17.2 1.1 %fusion.17 = f32[376,384]{1,0:T(8,128)S(1)} fusion(bf16[376,384]{1,0:T(8,128)(2,1)S(1)} %collective-permute-done.1, s32[376]{0:T(512)S(1)} %iota_add_fusion.1, s32[376]{0:T(512)} %param.9), kind=kOutput, calls=%fused_computation.34 | convolution fusion | flops 108718144 | bytes 869312 | tf_op jit(solution)/shard_map/dot_general | solution.py:94
  18.3 0.0 collective-permute-done
  18.3 0.0 copy-done.1
  18.3 0.5 fusion.3
  18.8 0.0 copy-start
  18.8 3.9 %collective-permute-start.3 = (f16[376,384]{1,0:T(8,128)(2,1)S(1)}, f16[376,384]{1,0:T(8,128)(2,1)S(1)}, u32[]{:S(2)}, u32[]{:S(2)}) collective-permute-start(f16[376,384]{1,0:T(8,128)(2,1)S(1)} %fusion.3), channel_id=1, source_target_pairs={{0,6},{1,7},{2,4},{3,5},{4,2},{5,3},{6,0},{7,1},{8,14},{9,15},{10,... | collective-permute-start | bytes 866312 | tf_op jit(solution)/shard_map/ppermute | solution.py:21
  22.7 0.1 pad_add_fusion.order_ref
  22.7 0.1 broadcast_in_dim.2
  22.8 0.1 collective-permute-start.9
  22.9 0.1 collective-permute-start.6
  23.0 0.1 fusion.13
  23.1 7.4 %collective-permute-done.3 = f16[376,384]{1,0:T(8,128)(2,1)S(1)} collective-permute-done((f16[376,384]{1,0:T(8,128)(2,1)S(1)}, f16[376,384]{1,0:T(8,128)(2,1)S(1)}, u32[]{:S(2)}, u32[]{:S(2)}) %collective-permute-start.3) | collective-permute-done | bytes 288800 | tf_op jit(solution)/shard_map/ppermute | solution.py:21
  30.5 0.0 collective-permute-start.8
  30.5 0.1 fusion.11
  30.6 5.4 %collective-permute-done.6 = f16[376,384]{1,0:T(8,128)(2,1)S(1)} collective-permute-done((f16[376,384]{1,0:T(8,128)(2,1)S(1)}, f16[376,384]{1,0:T(8,128)(2,1)S(1)}, u32[]{:S(2)}, u32[]{:S(2)}) %collective-permute-start.6) | collective-permute-done | bytes 288800 | tf_op jit(solution)/shard_map/ppermute | solution.py:21
  36.0 0.1 collective-permute-start.7
  36.1 0.1 fusion.9
  36.2 1.7 %collective-permute-start.4 = (f16[376,384]{1,0:T(8,128)(2,1)S(1)}, f16[376,384]{1,0:T(8,128)(2,1)S(1)}, u32[]{:S(2)}, u32[]{:S(2)}) collective-permute-start(f16[376,384]{1,0:T(8,128)(2,1)S(1)} %collective-permute-done.3), channel_id=1, source_target_pairs={{0,2},{1,3},{2,0},{3,1},{4,6},{5,7},{6,4},{7,5},{8,10},{9,11},{10,... | collective-permute-start | bytes 866312 | tf_op jit(solution)/shard_map/ppermute | solution.py:21
  37.8 0.0 collective-permute-done.9
  37.9 0.1 fusion.14
  37.9 0.0 copy-done
  38.0 1.9 %shard_map.55.refs_8_ = f32[376,384]{1,0:T(8,128)S(1)} custom-call(s32[2]{0:T(128)S(1)} %pad_add_fusion.1.order_ref, f32[24,384]{1,0:T(8,128)S(1)} %bitcast.16, bf16[376,384]{1,0:T(8,128)(2,1)S(1)} %get-tuple-element.8.refs_0_, bf16[376,384]{1,0:T(8,128)(2,1)S(1)} %get-tuple-element.7.refs_1_, bf16[376,384]{1,0:T(8,128)(2,1)S(1)} %get-tuple-element.6.refs_2_, ...), custom_call_target="tpu_custom_call" | custom-call | flops 443547648 | bytes 589824 | tf_op jit(solution)/shard_map/pallas_call | solution.py:63
  39.8 0.0 collective-permute-done.8
  39.8 0.1 fusion.12
  39.9 0.0 collective-permute-done.7
  39.9 0.1 fusion.10
  40.0 5.4 %collective-permute-done.4 = f16[376,384]{1,0:T(8,128)(2,1)S(1)} collective-permute-done((f16[376,384]{1,0:T(8,128)(2,1)S(1)}, f16[376,384]{1,0:T(8,128)(2,1)S(1)}, u32[]{:S(2)}, u32[]{:S(2)}) %collective-permute-start.4) | collective-permute-done | bytes 288800 | tf_op jit(solution)/shard_map/ppermute | solution.py:21
  45.4 0.0 collective-permute-start.5
  45.5 3.2 %shard_map.56.refs_2_ = f32[376,384]{1,0:T(8,128)S(1)} custom-call(s32[4]{0:T(128)S(1)} %pad_add_fusion.order_ref, f32[24,384]{1,0:T(8,128)S(1)} %bitcast.17, bf16[376,384]{1,0:T(8,128)(2,1)S(1)} %get-tuple-element.16.refs_0_, bf16[376,384]{1,0:T(8,128)(2,1)S(1)} %get-tuple-element.15.refs_1_, bf16[376,384]{1,0:T(8,128)(2,1)S(1)} %get-tuple-element.14.refs_2_, ...), custom_call_target="tpu_custom_call" | custom-call | flops 887095296 | bytes 1179648 | tf_op jit(solution)/shard_map/pallas_call | solution.py:63
  48.6 0.1 fusion.8
  48.7 0.6 %shard_map.57.refs_2_ = f32[376,384]{1,0:T(8,128)S(1)} custom-call(s32[1]{0:T(128)} %bitcast.1.order_ref, f32[24,384]{1,0:T(8,128)S(1)} %bitcast.18, bf16[376,384]{1,0:T(8,128)(2,1)S(1)} %get-tuple-element.18.refs_0_, bf16[376,384]{1,0:T(8,128)(2,1)S(1)} %get-tuple-element.17.refs_1_, f32[376,384]{1,0:T(8,128)S(1)} %shard_map.56.refs_2_, ...), custom_call_target="tpu_custom_call" | custom-call | flops 221773824 | bytes 294912 | tf_op jit(solution)/shard_map/pallas_call | solution.py:63
  49.4 0.0 collective-permute-done.5
  49.4 0.1 fusion.7
  49.5 1.4 %shard_map.58 = f32[376,384]{1,0:T(8,128)} custom-call(s32[1]{0:T(128)} %bitcast.order_ref, f32[24,384]{1,0:T(8,128)S(1)} %bitcast.19, bf16[376,384]{1,0:T(8,128)(2,1)S(1)} %get-tuple-element.20.refs_0_, bf16[376,384]{1,0:T(8,128)(2,1)S(1)} %get-tuple-element.19.refs_1_, f32[376,384]{1,0:T(8,128)S(1)} %shard_map.57.refs_2_, bf16[3072,384]{1,0:T(8,128)(2,1)S(1)} %copy-done), custom_call_target="tpu_custom_call" | custom-call | flops 221773824 | bytes 294912 | tf_op jit(solution)/shard_map/pallas_call | solution.py:63
  (5 shorter events, 0.0 us)
Async XLA Ops:
  0.0 18.3 %copy-start.1 = (s32[376]{0:T(512)S(1)}, s32[376]{0:T(512)}, u32[]{:S(2)}) copy-start(s32[376]{0:T(512)} %param.9) | copy-start | bytes 4516
  0.0 11.9 %collective-permute-start.2 = (bf16[376,384]{1,0:T(8,128)(2,1)}, bf16[376,384]{1,0:T(8,128)(2,1)S(1)}, u32[]{:S(2)}, u32[]{:S(2)}) collective-permute-start(bf16[376,384]{1,0:T(8,128)(2,1)} %param.5), channel_id=1, source_target_pairs={{0,24},{8,16},{16,8},{24,0},{1,25},{9,17},{17,9},{25,1},{2,26},{10... | collective-permute-start | bytes 866312 | tf_op jit(solution)/shard_map/ppermute | solution.py:97
  3.9 13.3 %collective-permute-start.1 = (bf16[376,384]{1,0:T(8,128)(2,1)}, bf16[376,384]{1,0:T(8,128)(2,1)S(1)}, u32[]{:S(2)}, u32[]{:S(2)}) collective-permute-start(bf16[376,384]{1,0:T(8,128)(2,1)} %param.5), channel_id=1, source_target_pairs={{0,16},{8,24},{16,0},{24,8},{1,17},{9,25},{17,1},{25,9},{2,18},{10... | collective-permute-start | bytes 866312 | tf_op jit(solution)/shard_map/ppermute | solution.py:97
  4.4 13.9 %collective-permute-start = (bf16[376,384]{1,0:T(8,128)(2,1)}, bf16[376,384]{1,0:T(8,128)(2,1)S(1)}, u32[]{:S(2)}, u32[]{:S(2)}) collective-permute-start(bf16[376,384]{1,0:T(8,128)(2,1)} %param.5), channel_id=1, source_target_pairs={{0,8},{8,0},{16,24},{24,16},{1,9},{9,1},{17,25},{25,17},{2,10},{10... | collective-permute-start | bytes 866312 | tf_op jit(solution)/shard_map/ppermute | solution.py:97
  18.8 19.2 %copy-start = (bf16[3072,384]{1,0:T(8,128)(2,1)S(1)}, bf16[3072,384]{1,0:T(8,128)(2,1)}, u32[]{:S(2)}) copy-start(bf16[3072,384]{1,0:T(8,128)(2,1)} %refs_3_.3) | copy-start | bytes 7077892
  18.8 11.7 %collective-permute-start.3 = (f16[376,384]{1,0:T(8,128)(2,1)S(1)}, f16[376,384]{1,0:T(8,128)(2,1)S(1)}, u32[]{:S(2)}, u32[]{:S(2)}) collective-permute-start(f16[376,384]{1,0:T(8,128)(2,1)S(1)} %fusion.3), channel_id=1, source_target_pairs={{0,6},{1,7},{2,4},{3,5},{4,2},{5,3},{6,0},{7,1},{8,14},{9,15},{10,... | collective-permute-start | bytes 866312 | tf_op jit(solution)/shard_map/ppermute | solution.py:21
  22.8 15.0 %collective-permute-start.9 = (f16[376,384]{1,0:T(8,128)(2,1)S(1)}, f16[376,384]{1,0:T(8,128)(2,1)S(1)}, u32[]{:S(2)}, u32[]{:S(2)}) collective-permute-start(f16[376,384]{1,0:T(8,128)(2,1)S(1)} %fusion.3), channel_id=1, source_target_pairs={{0,1},{1,0},{2,3},{3,2},{4,5},{5,4},{6,7},{7,6},{8,9},{9,8},{10,11... | collective-permute-start | bytes 866312 | tf_op jit(solution)/shard_map/ppermute | solution.py:21
  22.9 13.1 %collective-permute-start.6 = (f16[376,384]{1,0:T(8,128)(2,1)S(1)}, f16[376,384]{1,0:T(8,128)(2,1)S(1)}, u32[]{:S(2)}, u32[]{:S(2)}) collective-permute-start(f16[376,384]{1,0:T(8,128)(2,1)S(1)} %fusion.3), channel_id=1, source_target_pairs={{0,2},{1,3},{2,0},{3,1},{4,6},{5,7},{6,4},{7,5},{8,10},{9,11},{10,... | collective-permute-start | bytes 866312 | tf_op jit(solution)/shard_map/ppermute | solution.py:21
  30.5 9.3 %collective-permute-start.8 = (f16[376,384]{1,0:T(8,128)(2,1)S(1)}, f16[376,384]{1,0:T(8,128)(2,1)S(1)}, u32[]{:S(2)}, u32[]{:S(2)}) collective-permute-start(f16[376,384]{1,0:T(8,128)(2,1)S(1)} %collective-permute-done.3), channel_id=1, source_target_pairs={{0,1},{1,0},{2,3},{3,2},{4,5},{5,4},{6,7},{7,6},{8,9},{9,8},{10,11... | collective-permute-start | bytes 866312 | tf_op jit(solution)/shard_map/ppermute | solution.py:21
  36.0 3.9 %collective-permute-start.7 = (f16[376,384]{1,0:T(8,128)(2,1)S(1)}, f16[376,384]{1,0:T(8,128)(2,1)S(1)}, u32[]{:S(2)}, u32[]{:S(2)}) collective-permute-start(f16[376,384]{1,0:T(8,128)(2,1)S(1)} %collective-permute-done.6), channel_id=1, source_target_pairs={{0,1},{1,0},{2,3},{3,2},{4,5},{5,4},{6,7},{7,6},{8,9},{9,8},{10,11... | collective-permute-start | bytes 866312 | tf_op jit(solution)/shard_map/ppermute | solution.py:21
  36.2 9.3 %collective-permute-start.4 = (f16[376,384]{1,0:T(8,128)(2,1)S(1)}, f16[376,384]{1,0:T(8,128)(2,1)S(1)}, u32[]{:S(2)}, u32[]{:S(2)}) collective-permute-start(f16[376,384]{1,0:T(8,128)(2,1)S(1)} %collective-permute-done.3), channel_id=1, source_target_pairs={{0,2},{1,3},{2,0},{3,1},{4,6},{5,7},{6,4},{7,5},{8,10},{9,11},{10,... | collective-permute-start | bytes 866312 | tf_op jit(solution)/shard_map/ppermute | solution.py:21
  45.4 3.9 %collective-permute-start.5 = (f16[376,384]{1,0:T(8,128)(2,1)S(1)}, f16[376,384]{1,0:T(8,128)(2,1)S(1)}, u32[]{:S(2)}, u32[]{:S(2)}) collective-permute-start(f16[376,384]{1,0:T(8,128)(2,1)S(1)} %collective-permute-done.4), channel_id=1, source_target_pairs={{0,1},{1,0},{2,3},{3,2},{4,5},{5,4},{6,7},{7,6},{8,9},{9,8},{10,11... | collective-permute-start | bytes 866312 | tf_op jit(solution)/shard_map/ppermute | solution.py:21
where the time goes:
time: 51.1 us; the launch traced here: 50.9 us
  waiting for transfers between devices  26.5 us (52%)
  starting transfers between devices  10.3 us (20%)
  Pallas kernels  7.08 us (14%)
  matrix products  5.1 us (10%)
  other arithmetic  0.89 us (2%)
  local copies, waits for them, and re-layouts  0.83 us (2%)
    ppermute x7, waiting for transfers between devices, trade(): return lax.ppermute(values, 'vir', [(i, i ^ distance) for i in range(8)])  18.2 us
    ppermute x3, waiting for transfers between devices, body(): lax.ppermute(amplitudes, 'occ', [(i, i ^ k) for i in range(occ)])  8.23 us
    pallas_call x4, Pallas kernels, contract_body(): pl.pallas_call(functools.partial(contract_kernel, count, scale), out_shap...  7.08 us
    ppermute x7, starting transfers between devices, trade(): return lax.ppermute(values, 'vir', [(i, i ^ distance) for i in range(8)])  5.76 us
    ppermute x3, starting transfers between devices, body(): lax.ppermute(amplitudes, 'occ', [(i, i ^ k) for i in range(occ)])  4.55 us
    dot_general x4, matrix products, picked(): return jnp.dot(onehot, block, preferred_element_type=jnp.float32)  4.1 us
  transfers between devices with their start and end apart: 10, of which 5 were waited for; matrix products, arithmetic and copies ran while one was open for 12% of the time, Pallas kernels for 11%

commit v1 on v0

v1 whole, which is shorter than its diff:
```python
import functools

import jax
import jax.numpy as jnp
from jax import lax
from jax.experimental import pallas as pl
from jax.experimental.pallas import tpu as pltpu
from jax.sharding import PartitionSpec as P

TILE = 128
SCALE = 4096.0
CHUNKS = (2, 1)


def split(values):
    wide = values.astype(jnp.float32)
    high = lax.reduce_precision(wide, 8, 7)
    return high.astype(jnp.bfloat16), (wide - high).astype(jnp.bfloat16)


def trade(values, distance):
    return lax.ppermute(values, "vir", [(i, i ^ distance) for i in range(8)])


def cut_kernel(spans, source_ref, *refs):
    pieces, sems = refs[:-1], refs[-1]
    copies = []
    for i, (start, stop) in enumerate(spans):
        copies.append(
            pltpu.make_async_copy(source_ref.at[:, start:stop], pieces[i], sems.at[i])
        )
        copies[-1].start()
    for copy in copies:
        copy.wait()


def cut(source, spans):
    rows = source.shape[0]
    return pl.pallas_call(
        functools.partial(cut_kernel, spans),
        out_shape=[jax.ShapeDtypeStruct((rows, b - a), source.dtype) for a, b in spans],
        in_specs=[pl.BlockSpec(memory_space=pl.ANY)],
        out_specs=[pl.BlockSpec(memory_space=pltpu.VMEM)] * len(spans),
        scratch_shapes=[pltpu.SemaphoreType.DMA((len(spans),))],
        compiler_params=pltpu.CompilerParams(vmem_limit_bytes=4 << 20),
    )(source)


def masked_rows(block_ref, live_ref, first, at, depth):
    rows = []
    for t in range(depth // TILE):
        mask = live_ref[pl.ds(first + t, 1), :].astype(jnp.bfloat16)
        rows.append(block_ref[at + t * TILE : at + (t + 1) * TILE, :] * mask)
    return jnp.concatenate(rows, axis=0)


def contract_kernel(depths, ahead, has_base, origin_ref, live_ref, *refs):
    count = len(depths)
    pieces, refs = refs[: 2 * count], refs[2 * count :]
    if has_base:
        base_ref, refs = refs[0], refs[1:]
    integrals_ref, out_ref = refs[:2]
    kept, (block_ref, sems) = refs[2:-2], refs[-2:]
    copies, at = [], [0]
    for i, depth in enumerate(depths + ahead):
        start = pl.multiple_of(origin_ref[i] * TILE, TILE)
        copies.append(
            pltpu.make_async_copy(
                integrals_ref.at[pl.ds(start, depth), :],
                block_ref.at[pl.ds(at[-1], depth), :],
                sems.at[i],
            )
        )
        copies[-1].start()
        at.append(at[-1] + depth)
    total = base_ref[...] if has_base else None
    for i, depth in enumerate(depths):
        copies[i].wait()
        block = masked_rows(block_ref, live_ref, origin_ref[i], at[i], depth)
        for part in pieces[2 * i : 2 * i + 2]:
            term = jnp.dot(part[...], block, preferred_element_type=jnp.float32)
            total = term if total is None else total + term
    out_ref[...] = total
    for i, depth in enumerate(ahead):
        copies[count + i].wait()
        kept[i][...] = masked_rows(
            block_ref, live_ref, origin_ref[count + i], at[count + i], depth
        )


def contract(items, live, integrals, base=None, ahead=()):
    rows = items[0][0].shape[0]
    columns = integrals.shape[1]
    depths = tuple(item.shape[1] for item, _ in items)
    later = tuple(depth for _, depth in ahead)
    parts = [part for item, _ in items for part in split(item)]
    extra = [] if base is None else [base]
    tiles = [tile for _, tile in items] + [tile for tile, _ in ahead]
    vmem = pl.BlockSpec(memory_space=pltpu.VMEM)
    depth = sum(depths + later)
    return pl.pallas_call(
        functools.partial(contract_kernel, depths, later, base is not None),
        out_shape=[jax.ShapeDtypeStruct((rows, columns), jnp.float32)]
        + [jax.ShapeDtypeStruct((d, columns), jnp.bfloat16) for d in later],
        in_specs=[pl.BlockSpec(memory_space=pltpu.SMEM), vmem]
        + [vmem] * (len(parts) + len(extra))
        + [pl.BlockSpec(memory_space=pltpu.HBM)],
        out_specs=[vmem] * (1 + len(later)),
        scratch_shapes=[
            pltpu.VMEM((depth, columns), jnp.bfloat16),
            pltpu.SemaphoreType.DMA((len(tiles),)),
        ],
        compiler_params=pltpu.CompilerParams(vmem_limit_bytes=14 << 20),
        cost_estimate=pl.CostEstimate(
            flops=4 * rows * columns * sum(depths),
            transcendentals=0,
            bytes_accessed=2 * depth * columns,
        ),
    )(
        jnp.stack(tiles).astype(jnp.int32),
        live,
        *parts,
        *extra,
        pltpu.with_memory_space_constraint(integrals, pltpu.HBM),
    )


def finish_kernel(count, scale, *refs):
    pieces, blocks, base_ref, out_ref = refs[: 2 * count], refs[2 * count : -2], refs[-2], refs[-1]
    total = base_ref[...]
    for i in range(count):
        for part in pieces[2 * i : 2 * i + 2]:
            total = total + jnp.dot(
                part[...], blocks[i][...], preferred_element_type=jnp.float32
            )
    out_ref[...] = total if scale == 1.0 else total * scale


def finish(items, blocks, base, scale=1.0):
    parts = [part for item in items for part in split(item)]
    vmem = pl.BlockSpec(memory_space=pltpu.VMEM)
    return pl.pallas_call(
        functools.partial(finish_kernel, len(items), scale),
        out_shape=jax.ShapeDtypeStruct(base.shape, jnp.float32),
        in_specs=[vmem] * (len(parts) + len(blocks) + 1),
        out_specs=vmem,
        compiler_params=pltpu.CompilerParams(vmem_limit_bytes=14 << 20),
        cost_estimate=pl.CostEstimate(
            flops=4 * base.size * sum(item.shape[1] for item in items),
            transcendentals=0,
            bytes_accessed=4 * base.size,
        ),
    )(*parts, *blocks, base)


def body(amplitudes, integrals, tile_block, pair_mask, partner, occ, vir):
    rows, width = amplitudes.shape
    columns = integrals.shape[1]
    local_tiles = columns // TILE
    total_tiles = tile_block.shape[0]
    groups = pair_mask.shape[0]
    here = lax.axis_index("vir")
    me = lax.axis_index("occ")

    spans, at = [], 0
    for share in CHUNKS:
        spans.append((at, at + width * share // sum(CHUNKS)))
        at = spans[-1][1]
    chunks = range(len(spans))

    slots = jnp.arange(rows, dtype=jnp.int32)

    def chosen(source):
        onehot = (partner[:, None] == source * rows + slots[None, :]).astype(jnp.bfloat16)
        return lax.optimization_barrier(onehot)

    select = [chosen(me ^ hop) for hop in range(occ)]

    def picked(block, hop):
        return jnp.dot(select[hop], block, preferred_element_type=jnp.float32)

    pieces = list(cut(amplitudes, spans))
    differences, received = [], []
    for k in chunks:
        received.append(
            [
                lax.ppermute(pieces[k], "occ", [(i, i ^ hop) for i in range(occ)])
                for hop in range(1, occ)
            ]
        )
        differences.append(pieces[k].astype(jnp.float32) - picked(pieces[k], 0))
    sent = []
    for k, difference in enumerate(differences):
        for hop in range(1, occ):
            difference = difference - picked(received[k][hop - 1], hop)
        sent.append((difference * SCALE).astype(jnp.float16))

    labels = jnp.arange(groups, dtype=jnp.int32)
    own_blocks = lax.dynamic_slice_in_dim(tile_block, here * local_tiles, local_tiles)
    row_onehot = (tile_block[:, None] == labels[None, :]).astype(jnp.float32)
    col_onehot = (own_blocks[:, None] == labels[None, :]).astype(jnp.float32)
    live = jnp.dot(jnp.dot(row_onehot, pair_mask.astype(jnp.float32)), col_onehot.T)
    live = jnp.repeat(live, TILE, axis=1)

    if vir != 8:
        masked = integrals.reshape(total_tiles, TILE, columns)
        masked = masked * live.astype(jnp.bfloat16)[:, None, :]
        masked = masked.reshape(integrals.shape)
        whole = lax.all_gather(jnp.concatenate(sent, axis=1), "vir", axis=1, tiled=True)
        high, low = split(whole)
        total = jnp.dot(high, masked, preferred_element_type=jnp.float32)
        total = total + jnp.dot(low, masked, preferred_element_type=jnp.float32)
        return total * (1.0 / SCALE)

    plane, core = here // 2, here % 2

    def tile_of(k, step, other):
        shard = (plane ^ step) * 2 + (core ^ other)
        return shard * (width // TILE) + spans[k][0] // TILE

    def pair(k, item, step):
        return [
            (item, tile_of(k, step, 0)),
            (trade(item, 1), tile_of(k, step, 1)),
        ]

    own = [lax.optimization_barrier(item) for item in sent]
    third = [trade(own[k], 6) for k in chunks]
    first = [trade(own[k], 2) for k in chunks]
    second = [trade(third[k], 2) for k in chunks]

    early = [x for k in chunks for x in pair(k, own[k], 0)]
    middle = [x for k in chunks for x in pair(k, third[k], 3)]
    middle += [x for k in chunks for x in pair(k, first[k], 1)]
    late = [x for k in chunks for x in pair(k, second[k], 2)]
    ahead = [(tile, item.shape[1]) for item, tile in late]
    items = [item for item, _ in late]
    (total,) = contract(early, live, integrals)
    total, *blocks = contract(middle, live, integrals, total, ahead)
    total = finish(items[:-1], blocks[:-1], total)
    return finish(items[-1:], blocks[-1:], total, 1.0 / SCALE)


def solution(mesh):
    occ, vir = mesh.shape["occ"], mesh.shape["vir"]

    def whole(*args):
        return body(*args, occ, vir)

    placed = (P("occ", "vir"), P(None, "vir"), P(), P(), P("occ"))
    return jax.shard_map(
        whole, mesh=mesh, in_specs=placed, out_specs=P("occ", "vir"), check_vma=False
    )
```

time: 51.1 us -> 55.9 us (1.094)
  starting transfers between devices: 10.3 us -> 20.9 us
  waiting for transfers between devices: 26.5 us -> 19.6 us
  matrix products: 5.1 us -> 2.34 us
  Pallas kernels: 7.08 us -> 9.4 us
  other arithmetic: 0.89 us -> 1.8 us
    ppermute x7 -> x14, waiting for transfers between devices: 18.2 us -> 11.9 us  [trade(): return lax.ppermute(values, 'vir', [(i, i ^ distance) for i in range(8)])]
    ppermute x7 -> x14, starting transfers between devices: 5.76 us -> 11.4 us  [trade(): return lax.ppermute(values, 'vir', [(i, i ^ distance) for i in range(8)])]
    ppermute x3 -> x6, starting transfers between devices: 4.55 us -> 9.47 us  [body(): lax.ppermute(pieces[k], 'occ', [(i, i ^ hop) for i in range(occ)])]
    pallas_call x4 -> x5, Pallas kernels: 7.08 us -> 9.4 us  [the longest x2 7.48 us: contract(): pl.pallas_call(functools.partial(contract_kernel, depths, later, base is...]
    dot_general x4 -> x8, matrix products: 4.1 us -> 2.04 us  [picked(): return jnp.dot(select[hop], block, preferred_element_type=jnp.float32)]
    unnamed x5 -> x7, local copies, waits for them, and re-layouts: 0.01 us -> 0.97 us
    convert_element_type x0 -> x1, other arithmetic: none -> 0.94 us  [chosen(): (partner[:, None] == source * rows + slots[None, :]).astype(jnp.bfloat16)]
    dot_general x1, matrix products: 1 us -> 0.3 us  [body(): jnp.dot(jnp.dot(row_onehot, pair_mask.astype(jnp.float32)), col_onehot.T)]
  transfers between devices with their start and end apart: 10 -> 20, of which waited for: 5 -> 7; matrix products, arithmetic and copies ran while one was open for 12% -> 8% of each run, Pallas kernels for 11% -> 13%
where the time goes in v1:
time: 55.9 us; the launch traced here: 55.7 us
  starting transfers between devices  20.9 us (37%)
  waiting for transfers between devices  19.6 us (35%)
  Pallas kernels  9.4 us (17%)
  matrix products  2.34 us (4%)
  other arithmetic  1.8 us (3%)
  local copies, waits for them, and re-layouts  1.22 us (2%)
    ppermute x14, waiting for transfers between devices, trade(): return lax.ppermute(values, 'vir', [(i, i ^ distance) for i in range(8)])  11.9 us
    ppermute x14, starting transfers between devices, trade(): return lax.ppermute(values, 'vir', [(i, i ^ distance) for i in range(8)])  11.4 us
    ppermute x6, starting transfers between devices, body(): lax.ppermute(pieces[k], 'occ', [(i, i ^ hop) for i in range(occ)])  9.47 us
    ppermute x6, waiting for transfers between devices, body(): lax.ppermute(pieces[k], 'occ', [(i, i ^ hop) for i in range(occ)])  7.78 us
    pallas_call x2, Pallas kernels, contract(): pl.pallas_call(functools.partial(contract_kernel, depths, later, base is...  7.48 us
    dot_general x8, matrix products, picked(): return jnp.dot(select[hop], block, preferred_element_type=jnp.float32)  2.04 us
    pallas_call x2, Pallas kernels, finish(): pl.pallas_call(functools.partial(finish_kernel, len(items), scale), out_s...  1.86 us
  transfers between devices with their start and end apart: 20, of which 7 were waited for; matrix products, arithmetic and copies ran while one was open for 8% of the time, Pallas kernels for 13%

profile of v1, /device:TPU:0, one launch (start us, length us, event | category | flops | bytes accessed | tf_op | source)
XLA Modules:
  0.0 55.7 jit_solution(6346845510994652356)
XLA Ops:
  0.0 1.0 %copy-done = bf16[376,384]{1,0:T(8,128)(2,1)S(1)} copy-done((bf16[376,384]{1,0:T(8,128)(2,1)S(1)}, bf16[376,384]{1,0:T(8,128)(2,1)}, u32[]{:S(2)}) %copy-start) | copy-done | bytes 288792
  1.0 0.1 shard_map.55
  1.0 3.1 %collective-permute-start.7 = (bf16[376,256]{1,0:T(8,128)(2,1)S(1)}, bf16[376,256]{1,0:T(8,128)(2,1)S(1)}, u32[]{:S(2)}, u32[]{:S(2)}) collective-permute-start(bf16[376,256]{1,0:T(8,128)(2,1)S(1)} %get-tuple-element.13), channel_id=1, source_target_pairs={{0,16},{8,24},{16,0},{24,8},{1,17},{9,25},{17,1},{25,9},{2,18},{10... | collective-permute-start | bytes 577544 | tf_op jit(solution)/shard_map/ppermute | solution.py:187
  4.1 1.4 %collective-permute-start.8 = (bf16[376,256]{1,0:T(8,128)(2,1)S(1)}, bf16[376,256]{1,0:T(8,128)(2,1)S(1)}, u32[]{:S(2)}, u32[]{:S(2)}) collective-permute-start(bf16[376,256]{1,0:T(8,128)(2,1)S(1)} %get-tuple-element.13), channel_id=1, source_target_pairs={{0,24},{8,16},{16,8},{24,0},{1,25},{9,17},{17,9},{25,1},{2,26},{10... | collective-permute-start | bytes 577544 | tf_op jit(solution)/shard_map/ppermute | solution.py:187
  5.5 0.1 collective-permute-start.6
  5.6 1.9 %collective-permute-start.1 = (bf16[376,128]{1,0:T(8,128)(2,1)S(1)}, bf16[376,128]{1,0:T(8,128)(2,1)S(1)}, u32[]{:S(2)}, u32[]{:S(2)}) collective-permute-start(bf16[376,128]{1,0:T(8,128)(2,1)S(1)} %get-tuple-element.12), channel_id=1, source_target_pairs={{0,16},{8,24},{16,0},{24,8},{1,17},{9,25},{17,1},{25,9},{2,18},{10... | collective-permute-start | bytes 288776 | tf_op jit(solution)/shard_map/ppermute | solution.py:187
  7.6 1.4 %collective-permute-start.2 = (bf16[376,128]{1,0:T(8,128)(2,1)S(1)}, bf16[376,128]{1,0:T(8,128)(2,1)S(1)}, u32[]{:S(2)}, u32[]{:S(2)}) collective-permute-start(bf16[376,128]{1,0:T(8,128)(2,1)S(1)} %get-tuple-element.12), channel_id=1, source_target_pairs={{0,24},{8,16},{16,8},{24,0},{1,25},{9,17},{17,9},{25,1},{2,26},{10... | collective-permute-start | bytes 288776 | tf_op jit(solution)/shard_map/ppermute | solution.py:187
  9.0 0.9 %compare_convert_fusion.2 = (bf16[376,376]{1,0:T(8,128)(2,1)S(1)}, bf16[376,376]{1,0:T(8,128)(2,1)S(1)}, bf16[376,376]{1,0:T(8,128)(2,1)S(1)}, bf16[376,376]{1,0:T(8,128)(2,1)S(1)}) fusion(s32[376]{0:T(512)S(1)} %get-tuple-element.57, s32[376]{0:T(512)} %param.9, s32[376]{0:T(512)S(1)} %get-tuple-element.56, s32[376]{0:T(512)S(1)} %get-tuple-element.55, ...), kind=kLoop, calls=%fused_computation.16 | loop fusion | flops 1131008 | bytes 1138528 | tf_op jit(solution)/shard_map/convert_element_type | solution.py:174
  10.0 0.3 convolution_subtract_fusion.1
  10.2 0.3 convolution_subtract_fusion.3
  10.5 0.1 dynamic_slice.3
  10.6 0.3 fusion.8
  10.9 0.1 broadcast_in_dim.2
  11.1 0.1 stack.66.origin_ref
  11.1 0.1 pad_add_fusion.origin_ref
  11.2 5.2 %collective-permute-done.1 = bf16[376,128]{1,0:T(8,128)(2,1)S(1)} collective-permute-done((bf16[376,128]{1,0:T(8,128)(2,1)S(1)}, bf16[376,128]{1,0:T(8,128)(2,1)S(1)}, u32[]{:S(2)}, u32[]{:S(2)}) %collective-permute-start.1) | collective-permute-done | bytes 96288 | tf_op jit(solution)/shard_map/ppermute | solution.py:187
  16.4 1.5 %collective-permute-start = (bf16[376,128]{1,0:T(8,128)(2,1)S(1)}, bf16[376,128]{1,0:T(8,128)(2,1)S(1)}, u32[]{:S(2)}, u32[]{:S(2)}) collective-permute-start(bf16[376,128]{1,0:T(8,128)(2,1)S(1)} %get-tuple-element.12), channel_id=1, source_target_pairs={{0,8},{8,0},{16,24},{24,16},{1,9},{9,1},{17,25},{25,17},{2,10},{10... | collective-permute-start | bytes 288776 | tf_op jit(solution)/shard_map/ppermute | solution.py:187
  17.9 0.2 fusion.32
  18.2 0.0 collective-permute-done.2
  18.2 0.3 fusion.33
  18.4 2.6 %collective-permute-done = bf16[376,128]{1,0:T(8,128)(2,1)S(1)} collective-permute-done((bf16[376,128]{1,0:T(8,128)(2,1)S(1)}, bf16[376,128]{1,0:T(8,128)(2,1)S(1)}, u32[]{:S(2)}, u32[]{:S(2)}) %collective-permute-start) | collective-permute-done | bytes 96288 | tf_op jit(solution)/shard_map/ppermute | solution.py:187
  21.0 0.3 fusion.7
  21.3 0.1 collective-permute-start.17
  21.3 3.7 %collective-permute-start.3 = (f16[376,128]{1,0:T(8,128)(2,1)S(1)}, f16[376,128]{1,0:T(8,128)(2,1)S(1)}, u32[]{:S(2)}, u32[]{:S(2)}) collective-permute-start(f16[376,128]{1,0:T(8,128)(2,1)S(1)} %fusion.7), channel_id=1, source_target_pairs={{0,6},{1,7},{2,4},{3,5},{4,2},{5,3},{6,0},{7,1},{8,14},{9,15},{10,... | collective-permute-start | bytes 288776 | tf_op jit(solution)/shard_map/ppermute | solution.py:22
  25.1 0.0 collective-permute-done.7
  25.1 0.1 collective-permute-start.14
  25.1 0.3 fusion.34
  25.4 0.0 collective-permute-done.8
  25.4 0.3 fusion.35
  25.7 0.0 collective-permute-done.6
  25.7 0.3 fusion.3
  26.0 0.2 collective-permute-start.16
  26.2 0.1 fusion.15
  26.2 0.8 %collective-permute-start.9 = (f16[376,256]{1,0:T(8,128)(2,1)S(1)}, f16[376,256]{1,0:T(8,128)(2,1)S(1)}, u32[]{:S(2)}, u32[]{:S(2)}) collective-permute-start(f16[376,256]{1,0:T(8,128)(2,1)S(1)} %fusion.3), channel_id=1, source_target_pairs={{0,6},{1,7},{2,4},{3,5},{4,2},{5,3},{6,0},{7,1},{8,14},{9,15},{10,... | collective-permute-start | bytes 577544 | tf_op jit(solution)/shard_map/ppermute | solution.py:22
  27.1 1.8 %collective-permute-done.3 = f16[376,128]{1,0:T(8,128)(2,1)S(1)} collective-permute-done((f16[376,128]{1,0:T(8,128)(2,1)S(1)}, f16[376,128]{1,0:T(8,128)(2,1)S(1)}, u32[]{:S(2)}, u32[]{:S(2)}) %collective-permute-start.3) | collective-permute-done | bytes 96288 | tf_op jit(solution)/shard_map/ppermute | solution.py:22
  28.9 1.3 %collective-permute-start.12 = (f16[376,256]{1,0:T(8,128)(2,1)S(1)}, f16[376,256]{1,0:T(8,128)(2,1)S(1)}, u32[]{:S(2)}, u32[]{:S(2)}) collective-permute-start(f16[376,256]{1,0:T(8,128)(2,1)S(1)} %fusion.3), channel_id=1, source_target_pairs={{0,2},{1,3},{2,0},{3,1},{4,6},{5,7},{6,4},{7,5},{8,10},{9,11},{10,... | collective-permute-start | bytes 577544 | tf_op jit(solution)/shard_map/ppermute | solution.py:22
  30.2 0.0 collective-permute-done.17
  30.2 0.1 collective-permute-start.11
  30.3 0.2 collective-permute-done.14
  30.5 2.2 %collective-permute-start.4 = (f16[376,128]{1,0:T(8,128)(2,1)S(1)}, f16[376,128]{1,0:T(8,128)(2,1)S(1)}, u32[]{:S(2)}, u32[]{:S(2)}) collective-permute-start(f16[376,128]{1,0:T(8,128)(2,1)S(1)} %collective-permute-done.3), channel_id=1, source_target_pairs={{0,2},{1,3},{2,0},{3,1},{4,6},{5,7},{6,4},{7,5},{8,10},{9,11},{10,... | collective-permute-start | bytes 288776 | tf_op jit(solution)/shard_map/ppermute | solution.py:22
  32.8 8.2 %collective-permute-done.4 = f16[376,128]{1,0:T(8,128)(2,1)S(1)} collective-permute-done((f16[376,128]{1,0:T(8,128)(2,1)S(1)}, f16[376,128]{1,0:T(8,128)(2,1)S(1)}, u32[]{:S(2)}, u32[]{:S(2)}) %collective-permute-start.4) | collective-permute-done | bytes 96288 | tf_op jit(solution)/shard_map/ppermute | solution.py:22
  40.9 0.0 collective-permute-start.15
  41.0 0.0 collective-permute-done.11
  41.0 0.6 %collective-permute-start.5 = (f16[376,128]{1,0:T(8,128)(2,1)S(1)}, f16[376,128]{1,0:T(8,128)(2,1)S(1)}, u32[]{:S(2)}, u32[]{:S(2)}) collective-permute-start(f16[376,128]{1,0:T(8,128)(2,1)S(1)} %collective-permute-done.4), channel_id=1, source_target_pairs={{0,1},{1,0},{2,3},{3,2},{4,5},{5,4},{6,7},{7,6},{8,9},{9,8},{10,11... | collective-permute-start | bytes 288776 | tf_op jit(solution)/shard_map/ppermute | solution.py:22
  41.6 0.6 %collective-permute-done.15 = f16[376,128]{1,0:T(8,128)(2,1)S(1)} collective-permute-done((f16[376,128]{1,0:T(8,128)(2,1)S(1)}, f16[376,128]{1,0:T(8,128)(2,1)S(1)}, u32[]{:S(2)}, u32[]{:S(2)}) %collective-permute-start.15) | collective-permute-done | bytes 96288 | tf_op jit(solution)/shard_map/ppermute | solution.py:22
  42.3 0.0 collective-permute-done.9
  42.3 0.2 collective-permute-start.10
  42.5 1.6 %collective-permute-start.18 = (f16[376,256]{1,0:T(8,128)(2,1)S(1)}, f16[376,256]{1,0:T(8,128)(2,1)S(1)}, u32[]{:S(2)}, u32[]{:S(2)}) collective-permute-start(f16[376,256]{1,0:T(8,128)(2,1)S(1)} %collective-permute-done.9), channel_id=1, source_target_pairs={{0,2},{1,3},{2,0},{3,1},{4,6},{5,7},{6,4},{7,5},{8,10},{9,11},{10,... | collective-permute-start | bytes 577544 | tf_op jit(solution)/shard_map/ppermute | solution.py:22
  44.1 0.1 fusion.11
  44.2 0.1 collective-permute-start.13
  44.4 0.1 fusion.13
  44.4 0.0 collective-permute-done.16
  44.4 0.1 fusion.16
  44.5 3.0 %shard_map.56.refs_16_ = f32[376,384]{1,0:T(8,128)S(1)} custom-call(s32[4]{0:T(128)S(1)} %pad_add_fusion.origin_ref, f32[24,384]{1,0:T(8,128)S(1)} %bitcast.36, bf16[376,256]{1,0:T(8,128)(2,1)S(1)} %get-tuple-element.26.refs_0_, bf16[376,256]{1,0:T(8,128)(2,1)S(1)} %get-tuple-element.25.refs_1_, bf16[376,256]{1,0:T(8,128)(2,1)S(1)} %get-tuple-element.24.refs_2_, ...), custom_call_target="tpu_custom_call" | custom-call | flops 443547648 | bytes 589824 | tf_op jit(solution)/shard_map/pallas_call | solution.py:101
  47.5 0.1 fusion.12
  47.6 0.0 collective-permute-done.13
  47.6 0.1 fusion.14
  47.7 4.5 %shard_map.57 = (f32[376,384]{1,0:T(8,128)S(1)}, bf16[256,384]{1,0:T(8,128)(2,1)S(1)}, bf16[256,384]{1,0:T(8,128)(2,1)S(1)}, bf16[128,384]{1,0:T(8,128)(2,1)S(1)}, bf16[128,384]{1,0:T(8,128)(2,1)S(1)}) custom-call(s32[12]{0:T(128)S(1)} %stack.66.origin_ref, f32[24,384]{1,0:T(8,128)S(1)} %bitcast.37, bf16[376,256]{1,0:T(8,128)(2,1)S(1)} %get-tuple-element.34.refs_0_, ...), custom_call_target="tpu_custom_call" | custom-call | flops 887095296 | bytes 1769472 | tf_op jit(solution)/shard_map/pallas_call | solution.py:101
  52.2 0.5 collective-permute-start.19
  52.7 0.1 fusion.17
  52.8 1.0 %collective-permute-done.19 = f16[376,256]{1,0:T(8,128)(2,1)S(1)} collective-permute-done((f16[376,256]{1,0:T(8,128)(2,1)S(1)}, f16[376,256]{1,0:T(8,128)(2,1)S(1)}, u32[]{:S(2)}, u32[]{:S(2)}) %collective-permute-start.19) | collective-permute-done | bytes 192544 | tf_op jit(solution)/shard_map/ppermute | solution.py:22
  53.8 0.1 fusion.18
  53.8 0.7 %shard_map.58.refs_3_ = f32[376,384]{1,0:T(8,128)S(1)} custom-call(bf16[376,256]{1,0:T(8,128)(2,1)S(1)} %get-tuple-element.22.refs_0_, bf16[376,256]{1,0:T(8,128)(2,1)S(1)} %get-tuple-element.21.refs_1_, bf16[376,256]{1,0:T(8,128)(2,1)S(1)} %get-tuple-element.20.refs_2_, bf16[376,256]{1,0:T(8,128)(2,1)S(1)} %get-tuple-element.19.refs_3_, ...), custom_call_target="tpu_custom_call" | custom-call | flops 369623040 | bytes 577536 | tf_op jit(solution)/shard_map/pallas_call | solution.py:142
  54.6 1.1 %shard_map.59 = f32[376,384]{1,0:T(8,128)} custom-call(bf16[376,128]{1,0:T(8,128)(2,1)S(1)} %get-tuple-element.50.refs_0_, bf16[376,128]{1,0:T(8,128)(2,1)S(1)} %get-tuple-element.49.refs_1_, bf16[128,384]{1,0:T(8,128)(2,1)S(1)} %get-tuple-element.14.refs_2_, f32[376,384]{1,0:T(8,128)S(1)} %shard_map.58.refs_3_), custom_call_target="tpu_custom_call" | custom-call | flops 73924608 | bytes 577536 | tf_op jit(solution)/shard_map/pallas_call | solution.py:142
  (20 shorter events, 0.3 us)
Async XLA Ops:
  0.0 1.0 %copy-start = (bf16[376,384]{1,0:T(8,128)(2,1)S(1)}, bf16[376,384]{1,0:T(8,128)(2,1)}, u32[]{:S(2)}) copy-start(bf16[376,384]{1,0:T(8,128)(2,1)} %source_ref.1) | copy-start | bytes 866308
  1.0 9.6 %copy-start.2 = (s32[24]{0:T(128)S(1)}, s32[24]{0:T(128)}, u32[]{:S(2)}) copy-start(s32[24]{0:T(128)} %param.7) | copy-start | bytes 292
  1.0 9.7 %copy-start.1 = (s32[6,6]{1,0:T(8,128)S(1)}, s32[6,6]{1,0:T(8,128)}, u32[]{:S(2)}) copy-start(s32[6,6]{1,0:T(8,128)} %param.8) | copy-start | bytes 436
  1.0 24.0 %collective-permute-start.7 = (bf16[376,256]{1,0:T(8,128)(2,1)S(1)}, bf16[376,256]{1,0:T(8,128)(2,1)S(1)}, u32[]{:S(2)}, u32[]{:S(2)}) collective-permute-start(bf16[376,256]{1,0:T(8,128)(2,1)S(1)} %get-tuple-element.13), channel_id=1, source_target_pairs={{0,16},{8,24},{16,0},{24,8},{1,17},{9,25},{17,1},{25,9},{2,18},{10... | collective-permute-start | bytes 577544 | tf_op jit(solution)/shard_map/ppermute | solution.py:187
  4.1 21.3 %collective-permute-start.8 = (bf16[376,256]{1,0:T(8,128)(2,1)S(1)}, bf16[376,256]{1,0:T(8,128)(2,1)S(1)}, u32[]{:S(2)}, u32[]{:S(2)}) collective-permute-start(bf16[376,256]{1,0:T(8,128)(2,1)S(1)} %get-tuple-element.13), channel_id=1, source_target_pairs={{0,24},{8,16},{16,8},{24,0},{1,25},{9,17},{17,9},{25,1},{2,26},{10... | collective-permute-start | bytes 577544 | tf_op jit(solution)/shard_map/ppermute | solution.py:187
  5.5 20.2 %collective-permute-start.6 = (bf16[376,256]{1,0:T(8,128)(2,1)S(1)}, bf16[376,256]{1,0:T(8,128)(2,1)S(1)}, u32[]{:S(2)}, u32[]{:S(2)}) collective-permute-start(bf16[376,256]{1,0:T(8,128)(2,1)S(1)} %get-tuple-element.13), channel_id=1, source_target_pairs={{0,8},{8,0},{16,24},{24,16},{1,9},{9,1},{17,25},{25,17},{2,10},{10... | collective-permute-start | bytes 577544 | tf_op jit(solution)/shard_map/ppermute | solution.py:187
  5.6 10.8 %collective-permute-start.1 = (bf16[376,128]{1,0:T(8,128)(2,1)S(1)}, bf16[376,128]{1,0:T(8,128)(2,1)S(1)}, u32[]{:S(2)}, u32[]{:S(2)}) collective-permute-start(bf16[376,128]{1,0:T(8,128)(2,1)S(1)} %get-tuple-element.12), channel_id=1, source_target_pairs={{0,16},{8,24},{16,0},{24,8},{1,17},{9,25},{17,1},{25,9},{2,18},{10... | collective-permute-start | bytes 288776 | tf_op jit(solution)/shard_map/ppermute | solution.py:187
  7.6 10.6 %collective-permute-start.2 = (bf16[376,128]{1,0:T(8,128)(2,1)S(1)}, bf16[376,128]{1,0:T(8,128)(2,1)S(1)}, u32[]{:S(2)}, u32[]{:S(2)}) collective-permute-start(bf16[376,128]{1,0:T(8,128)(2,1)S(1)} %get-tuple-element.12), channel_id=1, source_target_pairs={{0,24},{8,16},{16,8},{24,0},{1,25},{9,17},{17,9},{25,1},{2,26},{10... | collective-permute-start | bytes 288776 | tf_op jit(solution)/shard_map/ppermute | solution.py:187
  16.4 4.6 %collective-permute-start = (bf16[376,128]{1,0:T(8,128)(2,1)S(1)}, bf16[376,128]{1,0:T(8,128)(2,1)S(1)}, u32[]{:S(2)}, u32[]{:S(2)}) collective-permute-start(bf16[376,128]{1,0:T(8,128)(2,1)S(1)} %get-tuple-element.12), channel_id=1, source_target_pairs={{0,8},{8,0},{16,24},{24,16},{1,9},{9,1},{17,25},{25,17},{2,10},{10... | collective-permute-start | bytes 288776 | tf_op jit(solution)/shard_map/ppermute | solution.py:187
  21.3 8.9 %collective-permute-start.17 = (f16[376,128]{1,0:T(8,128)(2,1)S(1)}, f16[376,128]{1,0:T(8,128)(2,1)S(1)}, u32[]{:S(2)}, u32[]{:S(2)}) collective-permute-start(f16[376,128]{1,0:T(8,128)(2,1)S(1)} %fusion.7), channel_id=1, source_target_pairs={{0,1},{1,0},{2,3},{3,2},{4,5},{5,4},{6,7},{7,6},{8,9},{9,8},{10,11... | collective-permute-start | bytes 288776 | tf_op jit(solution)/shard_map/ppermute | solution.py:22
  21.3 7.5 %collective-permute-start.3 = (f16[376,128]{1,0:T(8,128)(2,1)S(1)}, f16[376,128]{1,0:T(8,128)(2,1)S(1)}, u32[]{:S(2)}, u32[]{:S(2)}) collective-permute-start(f16[376,128]{1,0:T(8,128)(2,1)S(1)} %fusion.7), channel_id=1, source_target_pairs={{0,6},{1,7},{2,4},{3,5},{4,2},{5,3},{6,0},{7,1},{8,14},{9,15},{10,... | collective-permute-start | bytes 288776 | tf_op jit(solution)/shard_map/ppermute | solution.py:22
  25.1 5.5 %collective-permute-start.14 = (f16[376,128]{1,0:T(8,128)(2,1)S(1)}, f16[376,128]{1,0:T(8,128)(2,1)S(1)}, u32[]{:S(2)}, u32[]{:S(2)}) collective-permute-start(f16[376,128]{1,0:T(8,128)(2,1)S(1)} %fusion.7), channel_id=1, source_target_pairs={{0,2},{1,3},{2,0},{3,1},{4,6},{5,7},{6,4},{7,5},{8,10},{9,11},{10,... | collective-permute-start | bytes 288776 | tf_op jit(solution)/shard_map/ppermute | solution.py:22
  26.0 18.5 %collective-permute-start.16 = (f16[376,256]{1,0:T(8,128)(2,1)S(1)}, f16[376,256]{1,0:T(8,128)(2,1)S(1)}, u32[]{:S(2)}, u32[]{:S(2)}) collective-permute-start(f16[376,256]{1,0:T(8,128)(2,1)S(1)} %fusion.3), channel_id=1, source_target_pairs={{0,1},{1,0},{2,3},{3,2},{4,5},{5,4},{6,7},{7,6},{8,9},{9,8},{10,11... | collective-permute-start | bytes 577544 | tf_op jit(solution)/shard_map/ppermute | solution.py:22
  26.2 16.0 %collective-permute-start.9 = (f16[376,256]{1,0:T(8,128)(2,1)S(1)}, f16[376,256]{1,0:T(8,128)(2,1)S(1)}, u32[]{:S(2)}, u32[]{:S(2)}) collective-permute-start(f16[376,256]{1,0:T(8,128)(2,1)S(1)} %fusion.3), channel_id=1, source_target_pairs={{0,6},{1,7},{2,4},{3,5},{4,2},{5,3},{6,0},{7,1},{8,14},{9,15},{10,... | collective-permute-start | bytes 577544 | tf_op jit(solution)/shard_map/ppermute | solution.py:22
  28.9 15.3 %collective-permute-start.12 = (f16[376,256]{1,0:T(8,128)(2,1)S(1)}, f16[376,256]{1,0:T(8,128)(2,1)S(1)}, u32[]{:S(2)}, u32[]{:S(2)}) collective-permute-start(f16[376,256]{1,0:T(8,128)(2,1)S(1)} %fusion.3), channel_id=1, source_target_pairs={{0,2},{1,3},{2,0},{3,1},{4,6},{5,7},{6,4},{7,5},{8,10},{9,11},{10,... | collective-permute-start | bytes 577544 | tf_op jit(solution)/shard_map/ppermute | solution.py:22
  30.2 10.8 %collective-permute-start.11 = (f16[376,128]{1,0:T(8,128)(2,1)S(1)}, f16[376,128]{1,0:T(8,128)(2,1)S(1)}, u32[]{:S(2)}, u32[]{:S(2)}) collective-permute-start(f16[376,128]{1,0:T(8,128)(2,1)S(1)} %collective-permute-done.3), channel_id=1, source_target_pairs={{0,1},{1,0},{2,3},{3,2},{4,5},{5,4},{6,7},{7,6},{8,9},{9,8},{10,11... | collective-permute-start | bytes 288776 | tf_op jit(solution)/shard_map/ppermute | solution.py:22
  30.5 10.4 %collective-permute-start.4 = (f16[376,128]{1,0:T(8,128)(2,1)S(1)}, f16[376,128]{1,0:T(8,128)(2,1)S(1)}, u32[]{:S(2)}, u32[]{:S(2)}) collective-permute-start(f16[376,128]{1,0:T(8,128)(2,1)S(1)} %collective-permute-done.3), channel_id=1, source_target_pairs={{0,2},{1,3},{2,0},{3,1},{4,6},{5,7},{6,4},{7,5},{8,10},{9,11},{10,... | collective-permute-start | bytes 288776 | tf_op jit(solution)/shard_map/ppermute | solution.py:22
  40.9 1.3 %collective-permute-start.15 = (f16[376,128]{1,0:T(8,128)(2,1)S(1)}, f16[376,128]{1,0:T(8,128)(2,1)S(1)}, u32[]{:S(2)}, u32[]{:S(2)}) collective-permute-start(f16[376,128]{1,0:T(8,128)(2,1)S(1)} %collective-permute-done.14), channel_id=1, source_target_pairs={{0,1},{1,0},{2,3},{3,2},{4,5},{5,4},{6,7},{7,6},{8,9},{9,8},{10,11... | collective-permute-start | bytes 288776 | tf_op jit(solution)/shard_map/ppermute | solution.py:22
  41.0 6.5 %collective-permute-start.5 = (f16[376,128]{1,0:T(8,128)(2,1)S(1)}, f16[376,128]{1,0:T(8,128)(2,1)S(1)}, u32[]{:S(2)}, u32[]{:S(2)}) collective-permute-start(f16[376,128]{1,0:T(8,128)(2,1)S(1)} %collective-permute-done.4), channel_id=1, source_target_pairs={{0,1},{1,0},{2,3},{3,2},{4,5},{5,4},{6,7},{7,6},{8,9},{9,8},{10,11... | collective-permute-start | bytes 288776 | tf_op jit(solution)/shard_map/ppermute | solution.py:22
  42.3 5.2 %collective-permute-start.10 = (f16[376,256]{1,0:T(8,128)(2,1)S(1)}, f16[376,256]{1,0:T(8,128)(2,1)S(1)}, u32[]{:S(2)}, u32[]{:S(2)}) collective-permute-start(f16[376,256]{1,0:T(8,128)(2,1)S(1)} %collective-permute-done.9), channel_id=1, source_target_pairs={{0,1},{1,0},{2,3},{3,2},{4,5},{5,4},{6,7},{7,6},{8,9},{9,8},{10,11... | collective-permute-start | bytes 577544 | tf_op jit(solution)/shard_map/ppermute | solution.py:22
  42.5 9.7 %collective-permute-start.18 = (f16[376,256]{1,0:T(8,128)(2,1)S(1)}, f16[376,256]{1,0:T(8,128)(2,1)S(1)}, u32[]{:S(2)}, u32[]{:S(2)}) collective-permute-start(f16[376,256]{1,0:T(8,128)(2,1)S(1)} %collective-permute-done.9), channel_id=1, source_target_pairs={{0,2},{1,3},{2,0},{3,1},{4,6},{5,7},{6,4},{7,5},{8,10},{9,11},{10,... | collective-permute-start | bytes 577544 | tf_op jit(solution)/shard_map/ppermute | solution.py:22
  44.2 3.4 %collective-permute-start.13 = (f16[376,256]{1,0:T(8,128)(2,1)S(1)}, f16[376,256]{1,0:T(8,128)(2,1)S(1)}, u32[]{:S(2)}, u32[]{:S(2)}) collective-permute-start(f16[376,256]{1,0:T(8,128)(2,1)S(1)} %collective-permute-done.12), channel_id=1, source_target_pairs={{0,1},{1,0},{2,3},{3,2},{4,5},{5,4},{6,7},{7,6},{8,9},{9,8},{10,11... | collective-permute-start | bytes 577544 | tf_op jit(solution)/shard_map/ppermute | solution.py:22
  52.2 1.6 %collective-permute-start.19 = (f16[376,256]{1,0:T(8,128)(2,1)S(1)}, f16[376,256]{1,0:T(8,128)(2,1)S(1)}, u32[]{:S(2)}, u32[]{:S(2)}) collective-permute-start(f16[376,256]{1,0:T(8,128)(2,1)S(1)} %collective-permute-done.18), channel_id=1, source_target_pairs={{0,1},{1,0},{2,3},{3,2},{4,5},{5,4},{6,7},{7,6},{8,9},{9,8},{10,11... | collective-permute-start | bytes 577544 | tf_op jit(solution)/shard_map/ppermute | solution.py:22

commit v2 on v1

v2 whole, which is shorter than its diff:
```python
import functools

import jax
import jax.numpy as jnp
from jax import lax
from jax.experimental import pallas as pl
from jax.experimental.pallas import tpu as pltpu
from jax.sharding import PartitionSpec as P

TILE = 128
SCALE = 4096.0
CHUNKS = (2, 1)
INPLACE = True
STEPS = 3


def split(values):
    wide = values.astype(jnp.float32)
    high = lax.reduce_precision(wide, 8, 7)
    return high.astype(jnp.bfloat16), (wide - high).astype(jnp.bfloat16)


def trade(values, distance):
    return lax.ppermute(values, "vir", [(i, i ^ distance) for i in range(8)])


def cut_kernel(spans, source_ref, *refs):
    pieces, sems = refs[:-1], refs[-1]
    copies = []
    for i, (start, stop) in enumerate(spans):
        copies.append(
            pltpu.make_async_copy(source_ref.at[:, start:stop], pieces[i], sems.at[i])
        )
        copies[-1].start()
    for copy in copies:
        copy.wait()


def cut(source, spans):
    rows = source.shape[0]
    return pl.pallas_call(
        functools.partial(cut_kernel, spans),
        out_shape=[jax.ShapeDtypeStruct((rows, b - a), source.dtype) for a, b in spans],
        in_specs=[pl.BlockSpec(memory_space=pl.ANY)],
        out_specs=[pl.BlockSpec(memory_space=pltpu.VMEM)] * len(spans),
        scratch_shapes=[pltpu.SemaphoreType.DMA((len(spans),))],
        compiler_params=pltpu.CompilerParams(vmem_limit_bytes=4 << 20),
    )(source)


def contract_kernel(depths, ahead, inner, has_base, scale, *refs):
    count, later = len(depths), len(ahead)
    if later:
        (origin_ref, live_ref, integrals_ref), refs = refs[:3], refs[3:]
        (block_ref, sems), refs = refs[-2:], refs[:-2]
    pieces, refs = refs[: 2 * count], refs[2 * count :]
    ready = count - inner
    blocks, refs = refs[:ready], refs[ready:]
    if has_base:
        base_ref, refs = refs[0], refs[1:]
    copies, at = [], [0]
    for i, depth in enumerate(ahead):
        start = pl.multiple_of(origin_ref[i] * TILE, TILE)
        copies.append(
            pltpu.make_async_copy(
                integrals_ref.at[pl.ds(start, depth), :],
                block_ref.at[pl.ds(at[-1], depth), :],
                sems.at[i],
            )
        )
        copies[-1].start()
        at.append(at[-1] + depth)

    def masked(i):
        copies[i].wait()
        rows = []
        for t in range(ahead[i] // TILE):
            mask = live_ref[pl.ds(origin_ref[i] + t, 1), :].astype(jnp.bfloat16)
            rows.append(block_ref[at[i] + t * TILE : at[i] + (t + 1) * TILE, :] * mask)
        return rows

    if count:
        total = base_ref[...] if has_base else None
        for i in range(count):
            block = blocks[i][...] if i < ready else jnp.concatenate(masked(i - ready))
            for part in pieces[2 * i : 2 * i + 2]:
                term = jnp.dot(part[...], block, preferred_element_type=jnp.float32)
                total = term if total is None else total + term
        refs[0][...] = total if scale == 1.0 else total * scale
        refs = refs[1:]
    for i in range(inner, later):
        for t, rows in enumerate(masked(i)):
            refs[i - inner][t * TILE : (t + 1) * TILE, :] = rows


def contract(shape, items, blocks, base=None, scale=1.0, ahead=(), source=None):
    rows, columns = shape
    depths = tuple(item.shape[1] for item in items)
    later = tuple(depth for _, depth in ahead)
    inner = len(items) - len(blocks) if items else 0
    vmem = pl.BlockSpec(memory_space=pltpu.VMEM)
    args, specs, out, scratch = [], [], [], []
    if ahead:
        live, integrals = source
        args = [
            jnp.stack([tile for tile, _ in ahead]).astype(jnp.int32),
            live,
            pltpu.with_memory_space_constraint(integrals, pltpu.HBM),
        ]
        specs = [pl.BlockSpec(memory_space=pltpu.SMEM), vmem, pl.BlockSpec(memory_space=pltpu.HBM)]
        scratch = [
            pltpu.VMEM((sum(later), columns), jnp.bfloat16),
            pltpu.SemaphoreType.DMA((len(later),)),
        ]
    args += [part for item in items for part in split(item)] + list(blocks)
    alias = {}
    if base is not None:
        if INPLACE and scale == 1.0:
            alias = {len(args): 0}
        args.append(base)
    specs += [vmem] * (len(args) - len(specs))
    if items:
        out.append(jax.ShapeDtypeStruct((rows, columns), jnp.float32))
    out += [jax.ShapeDtypeStruct((depth, columns), jnp.bfloat16) for depth in later[inner:]]
    return pl.pallas_call(
        functools.partial(contract_kernel, depths, later, inner, base is not None, scale),
        out_shape=out,
        in_specs=specs,
        out_specs=[vmem] * len(out),
        scratch_shapes=scratch,
        input_output_aliases=alias,
        compiler_params=pltpu.CompilerParams(vmem_limit_bytes=10 << 20),
        cost_estimate=pl.CostEstimate(
            flops=4 * rows * columns * sum(depths),
            transcendentals=0,
            bytes_accessed=8 * rows * columns,
        ),
    )(*args)


def finish_kernel(count, steps, *refs):
    pieces, blocks = refs[: 2 * count], refs[2 * count : 3 * count]
    base_ref, out_ref, sum_ref, sems = refs[3 * count :]
    copies = []
    for i, (start, stop) in enumerate(steps):
        rows = slice(start, stop)
        total = base_ref[rows, :]
        for j in range(count):
            for part in pieces[2 * j : 2 * j + 2]:
                total = total + jnp.dot(
                    part[rows, :], blocks[j][...], preferred_element_type=jnp.float32
                )
        sum_ref[rows, :] = total * (1.0 / SCALE)
        copies.append(pltpu.make_async_copy(sum_ref.at[rows, :], out_ref.at[rows, :], sems.at[i]))
        copies[-1].start()
    for copy in copies:
        copy.wait()


def finish(items, blocks, base):
    rows, columns = base.shape
    size = -(-rows // (8 * STEPS)) * 8
    steps = [(a, min(a + size, rows)) for a in range(0, rows, size)]
    vmem = pl.BlockSpec(memory_space=pltpu.VMEM)
    parts = [part for item in items for part in split(item)]
    return pl.pallas_call(
        functools.partial(finish_kernel, len(items), steps),
        out_shape=jax.ShapeDtypeStruct((rows, columns), jnp.float32),
        in_specs=[vmem] * (len(parts) + len(blocks) + 1),
        out_specs=pl.BlockSpec(memory_space=pltpu.HBM),
        scratch_shapes=[
            pltpu.VMEM((rows, columns), jnp.float32),
            pltpu.SemaphoreType.DMA((len(steps),)),
        ],
        compiler_params=pltpu.CompilerParams(vmem_limit_bytes=10 << 20),
    )(*parts, *blocks, base)


def body(amplitudes, integrals, tile_block, pair_mask, partner, occ, vir):
    rows, width = amplitudes.shape
    columns = integrals.shape[1]
    local_tiles = columns // TILE
    total_tiles = tile_block.shape[0]
    groups = pair_mask.shape[0]
    here = lax.axis_index("vir")
    me = lax.axis_index("occ")

    spans, at = [], 0
    for share in CHUNKS:
        spans.append((at, at + width * share // sum(CHUNKS)))
        at = spans[-1][1]
    chunks = range(len(spans))

    slots = jnp.arange(rows, dtype=jnp.int32)

    def chosen(source):
        onehot = (partner[:, None] == source * rows + slots[None, :]).astype(jnp.bfloat16)
        return lax.optimization_barrier(onehot)

    select = [chosen(me ^ hop) for hop in range(occ)]

    def picked(block, hop):
        return jnp.dot(select[hop], block, preferred_element_type=jnp.float32)

    pieces = list(cut(amplitudes, spans))
    differences, received = [], []
    for k in chunks:
        received.append(
            [
                lax.ppermute(pieces[k], "occ", [(i, i ^ hop) for i in range(occ)])
                for hop in range(1, occ)
            ]
        )
        differences.append(pieces[k].astype(jnp.float32) - picked(pieces[k], 0))
    sent = []
    for k, difference in enumerate(differences):
        for hop in range(1, occ):
            difference = difference - picked(received[k][hop - 1], hop)
        sent.append((difference * SCALE).astype(jnp.float16))

    labels = jnp.arange(groups, dtype=jnp.int32)
    own_blocks = lax.dynamic_slice_in_dim(tile_block, here * local_tiles, local_tiles)
    row_onehot = (tile_block[:, None] == labels[None, :]).astype(jnp.float32)
    col_onehot = (own_blocks[:, None] == labels[None, :]).astype(jnp.float32)
    live = jnp.dot(jnp.dot(row_onehot, pair_mask.astype(jnp.float32)), col_onehot.T)
    live = jnp.repeat(live, TILE, axis=1)

    if vir != 8:
        masked = integrals.reshape(total_tiles, TILE, columns)
        masked = masked * live.astype(jnp.bfloat16)[:, None, :]
        masked = masked.reshape(integrals.shape)
        whole = lax.all_gather(jnp.concatenate(sent, axis=1), "vir", axis=1, tiled=True)
        high, low = split(whole)
        total = jnp.dot(high, masked, preferred_element_type=jnp.float32)
        total = total + jnp.dot(low, masked, preferred_element_type=jnp.float32)
        return total * (1.0 / SCALE)

    plane, core = here // 2, here % 2

    def rows_for(step, start, depth):
        return [
            (((plane ^ step) * 2 + (core ^ c)) * (width // TILE) + start // TILE, depth)
            for c in (0, 1)
        ]

    def pair(item):
        return [item, trade(item, 1)]

    own = [lax.optimization_barrier(item) for item in sent]
    whole = jnp.concatenate(own, axis=1)
    third = [trade(own[k], 6) for k in chunks]
    first = [trade(own[k], 2) for k in chunks]
    second = [trade(third[k], 2) for k in chunks]

    shape, source = (rows, columns), (live, integrals)
    parts = [(a, b - a) for a, b in spans]
    for_middle = [x for step in (3, 1) for part in parts for x in rows_for(step, *part)]
    for_late = [rows_for(2, *part)[c] for c in (0, 1) for part in parts]
    blocks = contract(shape, [], [], ahead=rows_for(0, 0, width)[:1], source=source)
    total, *blocks = contract(
        shape, pair(whole), blocks, ahead=rows_for(0, 0, width)[1:] + for_middle, source=source
    )
    items = [x for k in chunks for x in pair(third[k])]
    items += [x for k in chunks for x in pair(first[k])]
    total, *blocks = contract(shape, items, blocks, total, ahead=for_late, source=source)
    count = len(chunks)
    swapped = [trade(second[k], 1) for k in chunks]
    (total,) = contract(shape, second, blocks[:count], total)
    return finish(swapped, blocks[count:], total)


def solution(mesh):
    occ, vir = mesh.shape["occ"], mesh.shape["vir"]

    def whole(*args):
        return body(*args, occ, vir)

    placed = (P("occ", "vir"), P(None, "vir"), P(), P(), P("occ"))
    return jax.shard_map(
        whole, mesh=mesh, in_specs=placed, out_specs=P("occ", "vir"), check_vma=False
    )
```

time: 55.9 us -> 45.8 us (0.82)
  waiting for transfers between devices: 19.6 us -> 8.94 us
  starting transfers between devices: 20.9 us -> 21.9 us
    ppermute x6, waiting for transfers between devices: 7.78 us -> 0.75 us  [body(): lax.ppermute(pieces[k], 'occ', [(i, i ^ hop) for i in range(occ)])]
    ppermute x14 -> x13, waiting for transfers between devices: 11.9 us -> 8.2 us  [trade(): return lax.ppermute(values, 'vir', [(i, i ^ distance) for i in range(8)])]
    ppermute x14 -> x13, starting transfers between devices: 11.4 us -> 13.8 us  [trade(): return lax.ppermute(values, 'vir', [(i, i ^ distance) for i in range(8)])]
    ppermute x6, starting transfers between devices: 9.47 us -> 8.1 us  [body(): lax.ppermute(pieces[k], 'occ', [(i, i ^ hop) for i in range(occ)])]
    pallas_call x4 -> x5, Pallas kernels: 9.35 us -> 8.92 us  [the longest x4 7.68 us: contract(): pl.pallas_call(functools.partial(contract_kernel, depths, later, inner, b...]
  transfers between devices with their start and end apart: 20 -> 19, of which waited for: 7 -> 5; matrix products, arithmetic and copies ran while one was open for 8% -> 10% of each run, Pallas kernels for 13% -> 17%
where the time goes in v2:
time: 45.8 us; the launch traced here: 45.6 us
  starting transfers between devices  21.9 us (48%)
  Pallas kernels  8.97 us (20%)
  waiting for transfers between devices  8.94 us (20%)
  matrix products  2.34 us (5%)
  other arithmetic  1.89 us (4%)
  local copies, waits for them, and re-layouts  1.22 us (3%)
    ppermute x13, starting transfers between devices, trade(): return lax.ppermute(values, 'vir', [(i, i ^ distance) for i in range(8)])  13.8 us
    ppermute x13, waiting for transfers between devices, trade(): return lax.ppermute(values, 'vir', [(i, i ^ distance) for i in range(8)])  8.2 us
    ppermute x6, starting transfers between devices, body(): lax.ppermute(pieces[k], 'occ', [(i, i ^ hop) for i in range(occ)])  8.1 us
    pallas_call x4, Pallas kernels, contract(): pl.pallas_call(functools.partial(contract_kernel, depths, later, inner, b...  7.68 us
    dot_general x8, matrix products, picked(): return jnp.dot(select[hop], block, preferred_element_type=jnp.float32)  2.05 us
    pallas_call x1, Pallas kernels, finish(): pl.pallas_call(functools.partial(finish_kernel, len(items), steps), out_s...  1.24 us
    unnamed x7, local copies, waits for them, and re-layouts  0.97 us
    convert_element_type x1, other arithmetic, chosen(): (partner[:, None] == source * rows + slots[None, :]).astype(jnp.bfloat16)  0.94 us
  transfers between devices with their start and end apart: 19, of which 5 were waited for; matrix products, arithmetic and copies ran while one was open for 10% of the time, Pallas kernels for 17%

profile of v2, /device:TPU:0, one launch (start us, length us, event | category | flops | bytes accessed | tf_op | source)
XLA Modules:
  0.0 45.6 jit_solution(14405615212224851021)
XLA Ops:
  0.0 1.0 %copy-done = bf16[376,384]{1,0:T(8,128)(2,1)S(1)} copy-done((bf16[376,384]{1,0:T(8,128)(2,1)S(1)}, bf16[376,384]{1,0:T(8,128)(2,1)}, u32[]{:S(2)}) %copy-start) | copy-done | bytes 288792
  1.0 0.1 shard_map.55
  1.0 3.1 %collective-permute-start.7 = (bf16[376,128]{1,0:T(8,128)(2,1)S(1)}, bf16[376,128]{1,0:T(8,128)(2,1)S(1)}, u32[]{:S(2)}, u32[]{:S(2)}) collective-permute-start(bf16[376,128]{1,0:T(8,128)(2,1)S(1)} %get-tuple-element.22), channel_id=1, source_target_pairs={{0,16},{8,24},{16,0},{24,8},{1,17},{9,25},{17,1},{25,9},{2,18},{10... | collective-permute-start | bytes 288776 | tf_op jit(solution)/shard_map/ppermute | solution.py:210
  4.1 1.4 %collective-permute-start.8 = (bf16[376,128]{1,0:T(8,128)(2,1)S(1)}, bf16[376,128]{1,0:T(8,128)(2,1)S(1)}, u32[]{:S(2)}, u32[]{:S(2)}) collective-permute-start(bf16[376,128]{1,0:T(8,128)(2,1)S(1)} %get-tuple-element.22), channel_id=1, source_target_pairs={{0,24},{8,16},{16,8},{24,0},{1,25},{9,17},{17,9},{25,1},{2,26},{10... | collective-permute-start | bytes 288776 | tf_op jit(solution)/shard_map/ppermute | solution.py:210
  5.5 0.1 collective-permute-start.6
  5.6 1.9 %collective-permute-start.1 = (bf16[376,256]{1,0:T(8,128)(2,1)S(1)}, bf16[376,256]{1,0:T(8,128)(2,1)S(1)}, u32[]{:S(2)}, u32[]{:S(2)}) collective-permute-start(bf16[376,256]{1,0:T(8,128)(2,1)S(1)} %get-tuple-element.21), channel_id=1, source_target_pairs={{0,16},{8,24},{16,0},{24,8},{1,17},{9,25},{17,1},{25,9},{2,18},{10... | collective-permute-start | bytes 577544 | tf_op jit(solution)/shard_map/ppermute | solution.py:210
  7.6 1.4 %collective-permute-start.2 = (bf16[376,256]{1,0:T(8,128)(2,1)S(1)}, bf16[376,256]{1,0:T(8,128)(2,1)S(1)}, u32[]{:S(2)}, u32[]{:S(2)}) collective-permute-start(bf16[376,256]{1,0:T(8,128)(2,1)S(1)} %get-tuple-element.21), channel_id=1, source_target_pairs={{0,24},{8,16},{16,8},{24,0},{1,25},{9,17},{17,9},{25,1},{2,26},{10... | collective-permute-start | bytes 577544 | tf_op jit(solution)/shard_map/ppermute | solution.py:210
  9.0 0.9 %compare_convert_fusion.2 = (bf16[376,376]{1,0:T(8,128)(2,1)S(1)}, bf16[376,376]{1,0:T(8,128)(2,1)S(1)}, bf16[376,376]{1,0:T(8,128)(2,1)S(1)}, bf16[376,376]{1,0:T(8,128)(2,1)S(1)}) fusion(s32[376]{0:T(512)S(1)} %get-tuple-element.71, s32[376]{0:T(512)} %param.9, s32[376]{0:T(512)S(1)} %get-tuple-element.70, s32[376]{0:T(512)S(1)} %get-tuple-element.69, ...), kind=kLoop, calls=%fused_computation.22 | loop fusion | flops 1131008 | bytes 1138528 | tf_op jit(solution)/shard_map/convert_element_type | solution.py:197
  10.0 0.3 convolution_subtract_fusion.3
  10.2 0.3 convolution_subtract_fusion.1
  10.5 0.1 dynamic_slice.3
  10.6 0.3 fusion.8
  10.9 0.1 broadcast_in_dim.2
  11.0 1.0 %shard_map.56.refs_7_ = bf16[384,384]{1,0:T(8,128)(2,1)S(1)} custom-call(s32[1]{0:T(128)} %bitcast.13.refs_0_, f32[24,384]{1,0:T(8,128)S(1)} %bitcast.34, bf16[3072,384]{1,0:T(8,128)(2,1)} %refs_2_.5), custom_call_target="tpu_custom_call" | custom-call | bytes 1155072 | tf_op jit(solution)/shard_map/pallas_call | solution.py:125
  12.1 0.1 stack.62.refs_0_
  12.1 0.1 pad_add_fusion.refs_0_
  12.2 0.0 collective-permute-done.7
  12.2 0.1 collective-permute-start
  12.3 0.2 fusion.32
  12.6 0.0 collective-permute-done.8
  12.6 0.2 fusion.33
  12.9 0.0 collective-permute-done.6
  12.9 0.3 fusion.7
  13.1 4.1 %collective-permute-start.9 = (f16[376,128]{1,0:T(8,128)(2,1)S(1)}, f16[376,128]{1,0:T(8,128)(2,1)S(1)}, u32[]{:S(2)}, u32[]{:S(2)}) collective-permute-start(f16[376,128]{1,0:T(8,128)(2,1)S(1)} %fusion.7), channel_id=1, source_target_pairs={{0,6},{1,7},{2,4},{3,5},{4,2},{5,3},{6,0},{7,1},{8,14},{9,15},{10,... | collective-permute-start | bytes 288776 | tf_op jit(solution)/shard_map/ppermute | solution.py:24
  17.2 0.0 collective-permute-start.16
  17.2 0.2 collective-permute-done.1
  17.4 0.3 fusion.30
  17.7 0.0 collective-permute-done.2
  17.7 0.3 fusion.31
  18.0 0.5 %collective-permute-done = bf16[376,256]{1,0:T(8,128)(2,1)S(1)} collective-permute-done((bf16[376,256]{1,0:T(8,128)(2,1)S(1)}, bf16[376,256]{1,0:T(8,128)(2,1)S(1)}, u32[]{:S(2)}, u32[]{:S(2)}) %collective-permute-start) | collective-permute-done | bytes 192544 | tf_op jit(solution)/shard_map/ppermute | solution.py:210
  18.5 0.3 fusion.3
  18.8 3.9 %collective-permute-start.3 = (f16[376,256]{1,0:T(8,128)(2,1)S(1)}, f16[376,256]{1,0:T(8,128)(2,1)S(1)}, u32[]{:S(2)}, u32[]{:S(2)}) collective-permute-start(f16[376,256]{1,0:T(8,128)(2,1)S(1)} %fusion.3), channel_id=1, source_target_pairs={{0,6},{1,7},{2,4},{3,5},{4,2},{5,3},{6,0},{7,1},{8,14},{9,15},{10,... | collective-permute-start | bytes 577544 | tf_op jit(solution)/shard_map/ppermute | solution.py:24
  22.7 0.0 collective-permute-start.14
  22.7 0.1 pad_maximum_fusion
  22.8 0.1 collective-permute-start.18
  22.8 0.0 collective-permute-done.9
  22.9 0.5 %collective-permute-start.13 = (f16[376,128]{1,0:T(8,128)(2,1)S(1)}, f16[376,128]{1,0:T(8,128)(2,1)S(1)}, u32[]{:S(2)}, u32[]{:S(2)}) collective-permute-start(f16[376,128]{1,0:T(8,128)(2,1)S(1)} %collective-permute-done.9), channel_id=1, source_target_pairs={{0,1},{1,0},{2,3},{3,2},{4,5},{5,4},{6,7},{7,6},{8,9},{9,8},{10,11... | collective-permute-start | bytes 288776 | tf_op jit(solution)/shard_map/ppermute | solution.py:24
  23.4 0.0 collective-permute-done.16
  23.4 2.1 %collective-permute-start.10 = (f16[376,128]{1,0:T(8,128)(2,1)S(1)}, f16[376,128]{1,0:T(8,128)(2,1)S(1)}, u32[]{:S(2)}, u32[]{:S(2)}) collective-permute-start(f16[376,128]{1,0:T(8,128)(2,1)S(1)} %collective-permute-done.9), channel_id=1, source_target_pairs={{0,2},{1,3},{2,0},{3,1},{4,6},{5,7},{6,4},{7,5},{8,10},{9,11},{10,... | collective-permute-start | bytes 288776 | tf_op jit(solution)/shard_map/ppermute | solution.py:24
  25.5 0.1 fusion.11
  25.6 7.2 %collective-permute-done.10 = f16[376,128]{1,0:T(8,128)(2,1)S(1)} collective-permute-done((f16[376,128]{1,0:T(8,128)(2,1)S(1)}, f16[376,128]{1,0:T(8,128)(2,1)S(1)}, u32[]{:S(2)}, u32[]{:S(2)}) %collective-permute-start.10) | collective-permute-done | bytes 96288 | tf_op jit(solution)/shard_map/ppermute | solution.py:24
  32.8 0.0 collective-permute-start.17
  32.9 0.0 collective-permute-done.13
  32.9 0.6 %collective-permute-start.11 = (f16[376,128]{1,0:T(8,128)(2,1)S(1)}, f16[376,128]{1,0:T(8,128)(2,1)S(1)}, u32[]{:S(2)}, u32[]{:S(2)}) collective-permute-start(f16[376,128]{1,0:T(8,128)(2,1)S(1)} %collective-permute-done.10), channel_id=1, source_target_pairs={{0,1},{1,0},{2,3},{3,2},{4,5},{5,4},{6,7},{7,6},{8,9},{9,8},{10,11... | collective-permute-start | bytes 288776 | tf_op jit(solution)/shard_map/ppermute | solution.py:24
  33.5 0.6 %collective-permute-done.17 = f16[376,128]{1,0:T(8,128)(2,1)S(1)} collective-permute-done((f16[376,128]{1,0:T(8,128)(2,1)S(1)}, f16[376,128]{1,0:T(8,128)(2,1)S(1)}, u32[]{:S(2)}, u32[]{:S(2)}) %collective-permute-start.17) | collective-permute-done | bytes 96288 | tf_op jit(solution)/shard_map/ppermute | solution.py:24
  34.2 0.0 collective-permute-done.3
  34.2 0.2 collective-permute-start.12
  34.4 0.1 fusion.14
  34.4 1.8 %collective-permute-start.4 = (f16[376,256]{1,0:T(8,128)(2,1)S(1)}, f16[376,256]{1,0:T(8,128)(2,1)S(1)}, u32[]{:S(2)}, u32[]{:S(2)}) collective-permute-start(f16[376,256]{1,0:T(8,128)(2,1)S(1)} %collective-permute-done.3), channel_id=1, source_target_pairs={{0,2},{1,3},{2,0},{3,1},{4,6},{5,7},{6,4},{7,5},{8,10},{9,11},{10,... | collective-permute-start | bytes 577544 | tf_op jit(solution)/shard_map/ppermute | solution.py:24
  36.2 0.1 collective-permute-start.15
  36.3 0.0 collective-permute-done.11
  36.3 0.1 fusion.16
  36.4 0.1 fusion.12
  36.5 2.8 %shard_map.57 = (f32[376,384]{1,0:T(8,128)S(1)}, bf16[256,384]{1,0:T(8,128)(2,1)S(1)}, bf16[256,384]{1,0:T(8,128)(2,1)S(1)}, bf16[128,384]{1,0:T(8,128)(2,1)S(1)...) custom-call(s32[9]{0:T(128)S(1)} %stack.62.refs_0_, ...), custom_call_target="tpu_custom_call" | custom-call | flops 443547648 | bytes 1155072 | tf_op jit(solution)/shard_map/pallas_call | solution.py:125
  39.3 0.0 collective-permute-done.12
  39.4 0.1 fusion.15
  39.4 0.1 fusion.17
  39.5 3.2 %shard_map.58 = (f32[376,384]{1,0:T(8,128)S(1)}, bf16[256,384]{1,0:T(8,128)(2,1)S(1)}, bf16[128,384]{1,0:T(8,128)(2,1)S(1)}, bf16[256,384]{1,0:T(8,128)(2,1)S(1)}, bf16[128,384]{1,0:T(8,128)(2,1)S(1)}) custom-call(s32[4]{0:T(128)S(1)} %pad_add_fusion.refs_0_, f32[24,384]{1,0:T(8,128)S(1)} %bitcast.36, ...), custom_call_target="tpu_custom_call", output_to_operand_aliasing={{0}: (27, {})} | custom-call | flops 887095296 | bytes 1155072 | tf_op jit(solution)/shard_map/pallas_call | solution.py:125
  42.7 0.5 %collective-permute-start.5 = (f16[376,256]{1,0:T(8,128)(2,1)S(1)}, f16[376,256]{1,0:T(8,128)(2,1)S(1)}, u32[]{:S(2)}, u32[]{:S(2)}) collective-permute-start(f16[376,256]{1,0:T(8,128)(2,1)S(1)} %collective-permute-done.4), channel_id=1, source_target_pairs={{0,1},{1,0},{2,3},{3,2},{4,5},{5,4},{6,7},{7,6},{8,9},{9,8},{10,11... | collective-permute-start | bytes 577544 | tf_op jit(solution)/shard_map/ppermute | solution.py:24
  43.2 0.1 fusion.18
  43.3 0.6 %shard_map.59.refs_6_ = f32[376,384]{1,0:T(8,128)S(1)} custom-call(bf16[376,256]{1,0:T(8,128)(2,1)S(1)} %get-tuple-element.42.refs_0_, bf16[376,256]{1,0:T(8,128)(2,1)S(1)} %get-tuple-element.41.refs_1_, bf16[376,128]{1,0:T(8,128)(2,1)S(1)} %get-tuple-element.54.refs_2_, ...), custom_call_target="tpu_custom_call", output_to_operand_aliasing={{}: (6, {})} | custom-call | flops 221773824 | bytes 1155072 | tf_op jit(solution)/shard_map/pallas_call | solution.py:125
  43.9 0.4 collective-permute-done.5
  44.3 0.1 fusion.13
  44.3 1.2 %shard_map.60 = f32[376,384]{1,0:T(8,128)} custom-call(bf16[376,256]{1,0:T(8,128)(2,1)S(1)} %get-tuple-element.52.refs_0_, bf16[376,256]{1,0:T(8,128)(2,1)S(1)} %get-tuple-element.51.refs_1_, bf16[376,128]{1,0:T(8,128)(2,1)S(1)} %get-tuple-element.64.refs_2_, bf16[376,128]{1,0:T(8,128)(2,1)S(1)} %get-tuple-element.63.refs_3_, ...), custom_call_target="tpu_custom_call" | custom-call | tf_op jit(solution)/shard_map/pallas_call | solution.py:166
  (18 shorter events, 0.2 us)
Async XLA Ops:
  0.0 1.0 %copy-start = (bf16[376,384]{1,0:T(8,128)(2,1)S(1)}, bf16[376,384]{1,0:T(8,128)(2,1)}, u32[]{:S(2)}) copy-start(bf16[376,384]{1,0:T(8,128)(2,1)} %source_ref.1) | copy-start | bytes 866308
  1.0 9.6 %copy-start.2 = (s32[24]{0:T(128)S(1)}, s32[24]{0:T(128)}, u32[]{:S(2)}) copy-start(s32[24]{0:T(128)} %param.7) | copy-start | bytes 292
  1.0 9.7 %copy-start.1 = (s32[6,6]{1,0:T(8,128)S(1)}, s32[6,6]{1,0:T(8,128)}, u32[]{:S(2)}) copy-start(s32[6,6]{1,0:T(8,128)} %param.8) | copy-start | bytes 436
  1.0 11.2 %collective-permute-start.7 = (bf16[376,128]{1,0:T(8,128)(2,1)S(1)}, bf16[376,128]{1,0:T(8,128)(2,1)S(1)}, u32[]{:S(2)}, u32[]{:S(2)}) collective-permute-start(bf16[376,128]{1,0:T(8,128)(2,1)S(1)} %get-tuple-element.22), channel_id=1, source_target_pairs={{0,16},{8,24},{16,0},{24,8},{1,17},{9,25},{17,1},{25,9},{2,18},{10... | collective-permute-start | bytes 288776 | tf_op jit(solution)/shard_map/ppermute | solution.py:210
  4.1 8.5 %collective-permute-start.8 = (bf16[376,128]{1,0:T(8,128)(2,1)S(1)}, bf16[376,128]{1,0:T(8,128)(2,1)S(1)}, u32[]{:S(2)}, u32[]{:S(2)}) collective-permute-start(bf16[376,128]{1,0:T(8,128)(2,1)S(1)} %get-tuple-element.22), channel_id=1, source_target_pairs={{0,24},{8,16},{16,8},{24,0},{1,25},{9,17},{17,9},{25,1},{2,26},{10... | collective-permute-start | bytes 288776 | tf_op jit(solution)/shard_map/ppermute | solution.py:210
  5.5 7.4 %collective-permute-start.6 = (bf16[376,128]{1,0:T(8,128)(2,1)S(1)}, bf16[376,128]{1,0:T(8,128)(2,1)S(1)}, u32[]{:S(2)}, u32[]{:S(2)}) collective-permute-start(bf16[376,128]{1,0:T(8,128)(2,1)S(1)} %get-tuple-element.22), channel_id=1, source_target_pairs={{0,8},{8,0},{16,24},{24,16},{1,9},{9,1},{17,25},{25,17},{2,10},{10... | collective-permute-start | bytes 288776 | tf_op jit(solution)/shard_map/ppermute | solution.py:210
  5.6 11.8 %collective-permute-start.1 = (bf16[376,256]{1,0:T(8,128)(2,1)S(1)}, bf16[376,256]{1,0:T(8,128)(2,1)S(1)}, u32[]{:S(2)}, u32[]{:S(2)}) collective-permute-start(bf16[376,256]{1,0:T(8,128)(2,1)S(1)} %get-tuple-element.21), channel_id=1, source_target_pairs={{0,16},{8,24},{16,0},{24,8},{1,17},{9,25},{17,1},{25,9},{2,18},{10... | collective-permute-start | bytes 577544 | tf_op jit(solution)/shard_map/ppermute | solution.py:210
  7.6 10.1 %collective-permute-start.2 = (bf16[376,256]{1,0:T(8,128)(2,1)S(1)}, bf16[376,256]{1,0:T(8,128)(2,1)S(1)}, u32[]{:S(2)}, u32[]{:S(2)}) collective-permute-start(bf16[376,256]{1,0:T(8,128)(2,1)S(1)} %get-tuple-element.21), channel_id=1, source_target_pairs={{0,24},{8,16},{16,8},{24,0},{1,25},{9,17},{17,9},{25,1},{2,26},{10... | collective-permute-start | bytes 577544 | tf_op jit(solution)/shard_map/ppermute | solution.py:210
  12.2 6.3 %collective-permute-start = (bf16[376,256]{1,0:T(8,128)(2,1)S(1)}, bf16[376,256]{1,0:T(8,128)(2,1)S(1)}, u32[]{:S(2)}, u32[]{:S(2)}) collective-permute-start(bf16[376,256]{1,0:T(8,128)(2,1)S(1)} %get-tuple-element.21), channel_id=1, source_target_pairs={{0,8},{8,0},{16,24},{24,16},{1,9},{9,1},{17,25},{25,17},{2,10},{10... | collective-permute-start | bytes 577544 | tf_op jit(solution)/shard_map/ppermute | solution.py:210
  13.1 9.7 %collective-permute-start.9 = (f16[376,128]{1,0:T(8,128)(2,1)S(1)}, f16[376,128]{1,0:T(8,128)(2,1)S(1)}, u32[]{:S(2)}, u32[]{:S(2)}) collective-permute-start(f16[376,128]{1,0:T(8,128)(2,1)S(1)} %fusion.7), channel_id=1, source_target_pairs={{0,6},{1,7},{2,4},{3,5},{4,2},{5,3},{6,0},{7,1},{8,14},{9,15},{10,... | collective-permute-start | bytes 288776 | tf_op jit(solution)/shard_map/ppermute | solution.py:24
  17.2 6.1 %collective-permute-start.16 = (f16[376,128]{1,0:T(8,128)(2,1)S(1)}, f16[376,128]{1,0:T(8,128)(2,1)S(1)}, u32[]{:S(2)}, u32[]{:S(2)}) collective-permute-start(f16[376,128]{1,0:T(8,128)(2,1)S(1)} %fusion.7), channel_id=1, source_target_pairs={{0,2},{1,3},{2,0},{3,1},{4,6},{5,7},{6,4},{7,5},{8,10},{9,11},{10,... | collective-permute-start | bytes 288776 | tf_op jit(solution)/shard_map/ppermute | solution.py:24
  18.8 15.4 %collective-permute-start.3 = (f16[376,256]{1,0:T(8,128)(2,1)S(1)}, f16[376,256]{1,0:T(8,128)(2,1)S(1)}, u32[]{:S(2)}, u32[]{:S(2)}) collective-permute-start(f16[376,256]{1,0:T(8,128)(2,1)S(1)} %fusion.3), channel_id=1, source_target_pairs={{0,6},{1,7},{2,4},{3,5},{4,2},{5,3},{6,0},{7,1},{8,14},{9,15},{10,... | collective-permute-start | bytes 577544 | tf_op jit(solution)/shard_map/ppermute | solution.py:24
  22.7 13.5 %collective-permute-start.14 = (f16[376,256]{1,0:T(8,128)(2,1)S(1)}, f16[376,256]{1,0:T(8,128)(2,1)S(1)}, u32[]{:S(2)}, u32[]{:S(2)}) collective-permute-start(f16[376,256]{1,0:T(8,128)(2,1)S(1)} %fusion.3), channel_id=1, source_target_pairs={{0,2},{1,3},{2,0},{3,1},{4,6},{5,7},{6,4},{7,5},{8,10},{9,11},{10,... | collective-permute-start | bytes 577544 | tf_op jit(solution)/shard_map/ppermute | solution.py:24
  22.8 13.6 %collective-permute-start.18 = (f16[376,384]{1,0:T(8,128)(2,1)S(1)}, f16[376,384]{1,0:T(8,128)(2,1)S(1)}, u32[]{:S(2)}, u32[]{:S(2)}) collective-permute-start(f16[376,384]{1,0:T(8,128)(2,1)S(1)} %pad_maximum_fusion), channel_id=1, source_target_pairs={{0,1},{1,0},{2,3},{3,2},{4,5},{5,4},{6,7},{7,6},{8,9},{9,8},{10,11... | collective-permute-start | bytes 866312 | tf_op jit(solution)/shard_map/ppermute | solution.py:24
  22.9 10.0 %collective-permute-start.13 = (f16[376,128]{1,0:T(8,128)(2,1)S(1)}, f16[376,128]{1,0:T(8,128)(2,1)S(1)}, u32[]{:S(2)}, u32[]{:S(2)}) collective-permute-start(f16[376,128]{1,0:T(8,128)(2,1)S(1)} %collective-permute-done.9), channel_id=1, source_target_pairs={{0,1},{1,0},{2,3},{3,2},{4,5},{5,4},{6,7},{7,6},{8,9},{9,8},{10,11... | collective-permute-start | bytes 288776 | tf_op jit(solution)/shard_map/ppermute | solution.py:24
  23.4 9.4 %collective-permute-start.10 = (f16[376,128]{1,0:T(8,128)(2,1)S(1)}, f16[376,128]{1,0:T(8,128)(2,1)S(1)}, u32[]{:S(2)}, u32[]{:S(2)}) collective-permute-start(f16[376,128]{1,0:T(8,128)(2,1)S(1)} %collective-permute-done.9), channel_id=1, source_target_pairs={{0,2},{1,3},{2,0},{3,1},{4,6},{5,7},{6,4},{7,5},{8,10},{9,11},{10,... | collective-permute-start | bytes 288776 | tf_op jit(solution)/shard_map/ppermute | solution.py:24
  32.8 1.3 %collective-permute-start.17 = (f16[376,128]{1,0:T(8,128)(2,1)S(1)}, f16[376,128]{1,0:T(8,128)(2,1)S(1)}, u32[]{:S(2)}, u32[]{:S(2)}) collective-permute-start(f16[376,128]{1,0:T(8,128)(2,1)S(1)} %collective-permute-done.16), channel_id=1, source_target_pairs={{0,1},{1,0},{2,3},{3,2},{4,5},{5,4},{6,7},{7,6},{8,9},{9,8},{10,11... | collective-permute-start | bytes 288776 | tf_op jit(solution)/shard_map/ppermute | solution.py:24
  32.9 3.4 %collective-permute-start.11 = (f16[376,128]{1,0:T(8,128)(2,1)S(1)}, f16[376,128]{1,0:T(8,128)(2,1)S(1)}, u32[]{:S(2)}, u32[]{:S(2)}) collective-permute-start(f16[376,128]{1,0:T(8,128)(2,1)S(1)} %collective-permute-done.10), channel_id=1, source_target_pairs={{0,1},{1,0},{2,3},{3,2},{4,5},{5,4},{6,7},{7,6},{8,9},{9,8},{10,11... | collective-permute-start | bytes 288776 | tf_op jit(solution)/shard_map/ppermute | solution.py:24
  34.2 5.2 %collective-permute-start.12 = (f16[376,256]{1,0:T(8,128)(2,1)S(1)}, f16[376,256]{1,0:T(8,128)(2,1)S(1)}, u32[]{:S(2)}, u32[]{:S(2)}) collective-permute-start(f16[376,256]{1,0:T(8,128)(2,1)S(1)} %collective-permute-done.3), channel_id=1, source_target_pairs={{0,1},{1,0},{2,3},{3,2},{4,5},{5,4},{6,7},{7,6},{8,9},{9,8},{10,11... | collective-permute-start | bytes 577544 | tf_op jit(solution)/shard_map/ppermute | solution.py:24
  34.4 8.3 %collective-permute-start.4 = (f16[376,256]{1,0:T(8,128)(2,1)S(1)}, f16[376,256]{1,0:T(8,128)(2,1)S(1)}, u32[]{:S(2)}, u32[]{:S(2)}) collective-permute-start(f16[376,256]{1,0:T(8,128)(2,1)S(1)} %collective-permute-done.3), channel_id=1, source_target_pairs={{0,2},{1,3},{2,0},{3,1},{4,6},{5,7},{6,4},{7,5},{8,10},{9,11},{10,... | collective-permute-start | bytes 577544 | tf_op jit(solution)/shard_map/ppermute | solution.py:24
  36.2 3.2 %collective-permute-start.15 = (f16[376,256]{1,0:T(8,128)(2,1)S(1)}, f16[376,256]{1,0:T(8,128)(2,1)S(1)}, u32[]{:S(2)}, u32[]{:S(2)}) collective-permute-start(f16[376,256]{1,0:T(8,128)(2,1)S(1)} %collective-permute-done.14), channel_id=1, source_target_pairs={{0,1},{1,0},{2,3},{3,2},{4,5},{5,4},{6,7},{7,6},{8,9},{9,8},{10,11... | collective-permute-start | bytes 577544 | tf_op jit(solution)/shard_map/ppermute | solution.py:24
  42.7 1.6 %collective-permute-start.5 = (f16[376,256]{1,0:T(8,128)(2,1)S(1)}, f16[376,256]{1,0:T(8,128)(2,1)S(1)}, u32[]{:S(2)}, u32[]{:S(2)}) collective-permute-start(f16[376,256]{1,0:T(8,128)(2,1)S(1)} %collective-permute-done.4), channel_id=1, source_target_pairs={{0,1},{1,0},{2,3},{3,2},{4,5},{5,4},{6,7},{7,6},{8,9},{9,8},{10,11... | collective-permute-start | bytes 577544 | tf_op jit(solution)/shard_map/ppermute | solution.py:24

commit v3 on v2

--- a/solution.py
+++ b/solution.py
@@ -11,7 +11,7 @@
 SCALE = 4096.0
 CHUNKS = (2, 1)
 INPLACE = True
-STEPS = 3
+STEPS = 6
 
 
 def split(values):
@@ -48,14 +48,13 @@
     )(source)
 
 
-def contract_kernel(depths, ahead, inner, has_base, scale, *refs):
+def contract_kernel(depths, ahead, has_base, scale, *refs):
     count, later = len(depths), len(ahead)
     if later:
         (origin_ref, live_ref, integrals_ref), refs = refs[:3], refs[3:]
         (block_ref, sems), refs = refs[-2:], refs[:-2]
     pieces, refs = refs[: 2 * count], refs[2 * count :]
-    ready = count - inner
-    blocks, refs = refs[:ready], refs[ready:]
+    blocks, refs = refs[:count], refs[count:]
     if has_base:
         base_ref, refs = refs[0], refs[1:]
     copies, at = [], [0]
@@ -70,34 +69,27 @@
         )
         copies[-1].start()
         at.append(at[-1] + depth)
-
-    def masked(i):
-        copies[i].wait()
-        rows = []
-        for t in range(ahead[i] // TILE):
-            mask = live_ref[pl.ds(origin_ref[i] + t, 1), :].astype(jnp.bfloat16)
-            rows.append(block_ref[at[i] + t * TILE : at[i] + (t + 1) * TILE, :] * mask)
-        return rows
-
     if count:
         total = base_ref[...] if has_base else None
         for i in range(count):
-            block = blocks[i][...] if i < ready else jnp.concatenate(masked(i - ready))
+            block = blocks[i][...]
             for part in pieces[2 * i : 2 * i + 2]:
                 term = jnp.dot(part[...], block, preferred_element_type=jnp.float32)
                 total = term if total is None else total + term
         refs[0][...] = total if scale == 1.0 else total * scale
         refs = refs[1:]
-    for i in range(inner, later):
-        for t, rows in enumerate(masked(i)):
-            refs[i - inner][t * TILE : (t + 1) * TILE, :] = rows
+    for i, depth in enumerate(ahead):
+        copies[i].wait()
+        for t in range(depth // TILE):
+            mask = live_ref[pl.ds(origin_ref[i] + t, 1), :].astype(jnp.bfloat16)
+            rows = slice(at[i] + t * TILE, at[i] + (t + 1) * TILE)
+            refs[i][t * TILE : (t + 1) * TILE, :] = block_ref[rows, :] * mask
 
 
 def contract(shape, items, blocks, base=None, scale=1.0, ahead=(), source=None):
     rows, columns = shape
     depths = tuple(item.shape[1] for item in items)
     later = tuple(depth for _, depth in ahead)
-    inner = len(items) - len(blocks) if items else 0
     vmem = pl.BlockSpec(memory_space=pltpu.VMEM)
     args, specs, out, scratch = [], [], [], []
     if ahead:
@@ -107,7 +99,11 @@
             live,
             pltpu.with_memory_space_constraint(integrals, pltpu.HBM),
         ]
-        specs = [pl.BlockSpec(memory_space=pltpu.SMEM), vmem, pl.BlockSpec(memory_space=pltpu.HBM)]
+        specs = [
+            pl.BlockSpec(memory_space=pltpu.SMEM),
+            vmem,
+            pl.BlockSpec(memory_space=pltpu.HBM),
+        ]
         scratch = [
             pltpu.VMEM((sum(later), columns), jnp.bfloat16),
             pltpu.SemaphoreType.DMA((len(later),)),
@@ -121,9 +117,9 @@
     specs += [vmem] * (len(args) - len(specs))
     if items:
         out.append(jax.ShapeDtypeStruct((rows, columns), jnp.float32))
-    out += [jax.ShapeDtypeStruct((depth, columns), jnp.bfloat16) for depth in later[inner:]]
+    out += [jax.ShapeDtypeStruct((depth, columns), jnp.bfloat16) for depth in later]
     return pl.pallas_call(
-        functools.partial(contract_kernel, depths, later, inner, base is not None, scale),
+        functools.partial(contract_kernel, depths, later, base is not None, scale),
         out_shape=out,
         in_specs=specs,
         out_specs=[vmem] * len(out),
@@ -256,13 +252,15 @@
     parts = [(a, b - a) for a, b in spans]
     for_middle = [x for step in (3, 1) for part in parts for x in rows_for(step, *part)]
     for_late = [rows_for(2, *part)[c] for c in (0, 1) for part in parts]
-    blocks = contract(shape, [], [], ahead=rows_for(0, 0, width)[:1], source=source)
+    blocks = contract(shape, [], [], ahead=rows_for(0, 0, width), source=source)
     total, *blocks = contract(
-        shape, pair(whole), blocks, ahead=rows_for(0, 0, width)[1:] + for_middle, source=source
+        shape, pair(whole), blocks, ahead=for_middle, source=source
     )
     items = [x for k in chunks for x in pair(third[k])]
     items += [x for k in chunks for x in pair(first[k])]
-    total, *blocks = contract(shape, items, blocks, total, ahead=for_late, source=source)
+    total, *blocks = contract(
+        shape, items, blocks, total, ahead=for_late, source=source
+    )
     count = len(chunks)
     swapped = [trade(second[k], 1) for k in chunks]
     (total,) = contract(shape, second, blocks[:count], total)

time: 45.8 us -> 45.5 us (level)
  starting transfers between devices: 21.9 us -> 19.3 us
  waiting for transfers between devices: 8.94 us -> 10.4 us
  Pallas kernels: 8.97 us -> 9.66 us
    ppermute x13, starting transfers between devices: 13.8 us -> 11.2 us  [trade(): return lax.ppermute(values, 'vir', [(i, i ^ distance) for i in range(8)])]
    ppermute x13, waiting for transfers between devices: 8.2 us -> 10.3 us  [trade(): return lax.ppermute(values, 'vir', [(i, i ^ distance) for i in range(8)])]
    ppermute x6, waiting for transfers between devices: 0.75 us -> 0.1 us  [body(): lax.ppermute(pieces[k], 'occ', [(i, i ^ hop) for i in range(occ)])]
    pallas_call x4, Pallas kernels: 7.68 us -> 8.2 us  [contract(): pl.pallas_call(functools.partial(contract_kernel, depths, later, base is...]
  transfers between devices with their start and end apart: 19 -> 19, of which waited for: 5 -> 5; matrix products, arithmetic and copies ran while one was open for 10% -> 10% of each run, Pallas kernels for 17% -> 18%
where the time goes in v3:
time: 45.5 us; the launch traced here: 45.2 us
  starting transfers between devices  19.3 us (42%)
  waiting for transfers between devices  10.4 us (23%)
  Pallas kernels  9.66 us (21%)
  matrix products  2.34 us (5%)
  other arithmetic  1.97 us (4%)
  local copies, waits for them, and re-layouts  1.22 us (3%)
    ppermute x13, starting transfers between devices, trade(): return lax.ppermute(values, 'vir', [(i, i ^ distance) for i in range(8)])  11.2 us
    ppermute x13, waiting for transfers between devices, trade(): return lax.ppermute(values, 'vir', [(i, i ^ distance) for i in range(8)])  10.3 us
    pallas_call x4, Pallas kernels, contract(): pl.pallas_call(functools.partial(contract_kernel, depths, later, base is...  8.2 us
    ppermute x6, starting transfers between devices, body(): lax.ppermute(pieces[k], 'occ', [(i, i ^ hop) for i in range(occ)])  8.1 us
    dot_general x8, matrix products, picked(): return jnp.dot(select[hop], block, preferred_element_type=jnp.float32)  2.04 us
    pallas_call x1, Pallas kernels, finish(): pl.pallas_call(functools.partial(finish_kernel, len(items), steps), out_s...  1.41 us
    unnamed x7, local copies, waits for them, and re-layouts  0.97 us
    convert_element_type x1, other arithmetic, chosen(): (partner[:, None] == source * rows + slots[None, :]).astype(jnp.bfloat16)  0.94 us
  transfers between devices with their start and end apart: 19, of which 5 were waited for; matrix products, arithmetic and copies ran while one was open for 10% of the time, Pallas kernels for 18%

profile of v3, /device:TPU:0, one launch (start us, length us, event | category | flops | bytes accessed | tf_op | source)
XLA Modules:
  0.0 45.2 jit_solution(13681515389558943239)
XLA Ops:
  0.0 1.0 %copy-done = bf16[376,384]{1,0:T(8,128)(2,1)S(1)} copy-done((bf16[376,384]{1,0:T(8,128)(2,1)S(1)}, bf16[376,384]{1,0:T(8,128)(2,1)}, u32[]{:S(2)}) %copy-start) | copy-done | bytes 288792
  1.0 0.1 shard_map.55
  1.0 3.1 %collective-permute-start.7 = (bf16[376,128]{1,0:T(8,128)(2,1)S(1)}, bf16[376,128]{1,0:T(8,128)(2,1)S(1)}, u32[]{:S(2)}, u32[]{:S(2)}) collective-permute-start(bf16[376,128]{1,0:T(8,128)(2,1)S(1)} %get-tuple-element.24), channel_id=1, source_target_pairs={{0,16},{8,24},{16,0},{24,8},{1,17},{9,25},{17,1},{25,9},{2,18},{10... | collective-permute-start | bytes 288776 | tf_op jit(solution)/shard_map/ppermute | solution.py:206
  4.1 1.4 %collective-permute-start.8 = (bf16[376,128]{1,0:T(8,128)(2,1)S(1)}, bf16[376,128]{1,0:T(8,128)(2,1)S(1)}, u32[]{:S(2)}, u32[]{:S(2)}) collective-permute-start(bf16[376,128]{1,0:T(8,128)(2,1)S(1)} %get-tuple-element.24), channel_id=1, source_target_pairs={{0,24},{8,16},{16,8},{24,0},{1,25},{9,17},{17,9},{25,1},{2,26},{10... | collective-permute-start | bytes 288776 | tf_op jit(solution)/shard_map/ppermute | solution.py:206
  5.5 0.1 collective-permute-start.6
  5.6 1.9 %collective-permute-start.1 = (bf16[376,256]{1,0:T(8,128)(2,1)S(1)}, bf16[376,256]{1,0:T(8,128)(2,1)S(1)}, u32[]{:S(2)}, u32[]{:S(2)}) collective-permute-start(bf16[376,256]{1,0:T(8,128)(2,1)S(1)} %get-tuple-element.23), channel_id=1, source_target_pairs={{0,16},{8,24},{16,0},{24,8},{1,17},{9,25},{17,1},{25,9},{2,18},{10... | collective-permute-start | bytes 577544 | tf_op jit(solution)/shard_map/ppermute | solution.py:206
  7.6 1.4 %collective-permute-start.2 = (bf16[376,256]{1,0:T(8,128)(2,1)S(1)}, bf16[376,256]{1,0:T(8,128)(2,1)S(1)}, u32[]{:S(2)}, u32[]{:S(2)}) collective-permute-start(bf16[376,256]{1,0:T(8,128)(2,1)S(1)} %get-tuple-element.23), channel_id=1, source_target_pairs={{0,24},{8,16},{16,8},{24,0},{1,25},{9,17},{17,9},{25,1},{2,26},{10... | collective-permute-start | bytes 577544 | tf_op jit(solution)/shard_map/ppermute | solution.py:206
  9.0 0.9 %compare_convert_fusion.2 = (bf16[376,376]{1,0:T(8,128)(2,1)S(1)}, bf16[376,376]{1,0:T(8,128)(2,1)S(1)}, bf16[376,376]{1,0:T(8,128)(2,1)S(1)}, bf16[376,376]{1,0:T(8,128)(2,1)S(1)}) fusion(s32[376]{0:T(512)S(1)} %get-tuple-element.75, s32[376]{0:T(512)} %param.9, s32[376]{0:T(512)S(1)} %get-tuple-element.74, s32[376]{0:T(512)S(1)} %get-tuple-element.73, ...), kind=kLoop, calls=%fused_computation.22 | loop fusion | flops 1131008 | bytes 1138528 | tf_op jit(solution)/shard_map/convert_element_type | solution.py:193
  10.0 0.3 convolution_subtract_fusion.3
  10.2 0.3 convolution_subtract_fusion.1
  10.5 0.1 dynamic_slice.3
  10.6 0.3 fusion.8
  10.9 0.1 broadcast_in_dim.2
  11.0 0.1 pad_add_fusion.1.refs_0_
  11.1 1.6 %shard_map.56 = (bf16[384,384]{1,0:T(8,128)(2,1)S(1)}, bf16[384,384]{1,0:T(8,128)(2,1)S(1)}) custom-call(s32[2]{0:T(128)S(1)} %pad_add_fusion.1.refs_0_, f32[24,384]{1,0:T(8,128)S(1)} %bitcast.34, bf16[3072,384]{1,0:T(8,128)(2,1)} %refs_2_.5), custom_call_target="tpu_custom_call" | custom-call | bytes 1155072 | tf_op jit(solution)/shard_map/pallas_call | solution.py:121
  12.8 0.1 stack.64.refs_0_
  12.9 0.1 pad_add_fusion.refs_0_
  12.9 0.0 collective-permute-done.7
  12.9 0.1 collective-permute-start
  13.1 0.3 fusion.32
  13.3 0.0 collective-permute-done.8
  13.3 0.2 fusion.33
  13.6 0.0 collective-permute-done.6
  13.6 0.3 fusion.7
  13.9 4.1 %collective-permute-start.9 = (f16[376,128]{1,0:T(8,128)(2,1)S(1)}, f16[376,128]{1,0:T(8,128)(2,1)S(1)}, u32[]{:S(2)}, u32[]{:S(2)}) collective-permute-start(f16[376,128]{1,0:T(8,128)(2,1)S(1)} %fusion.7), channel_id=1, source_target_pairs={{0,6},{1,7},{2,4},{3,5},{4,2},{5,3},{6,0},{7,1},{8,14},{9,15},{10,... | collective-permute-start | bytes 288776 | tf_op jit(solution)/shard_map/ppermute | solution.py:24
  17.9 0.0 collective-permute-start.16
  18.0 0.0 collective-permute-done.1
  18.0 0.3 fusion.30
  18.2 0.0 collective-permute-done.2
  18.2 0.3 fusion.31
  18.5 0.1 collective-permute-done
  18.6 0.3 fusion.3
  18.8 3.8 %collective-permute-start.3 = (f16[376,256]{1,0:T(8,128)(2,1)S(1)}, f16[376,256]{1,0:T(8,128)(2,1)S(1)}, u32[]{:S(2)}, u32[]{:S(2)}) collective-permute-start(f16[376,256]{1,0:T(8,128)(2,1)S(1)} %fusion.3), channel_id=1, source_target_pairs={{0,6},{1,7},{2,4},{3,5},{4,2},{5,3},{6,0},{7,1},{8,14},{9,15},{10,... | collective-permute-start | bytes 577544 | tf_op jit(solution)/shard_map/ppermute | solution.py:24
  22.7 0.0 collective-permute-start.14
  22.7 0.1 pad_maximum_fusion
  22.8 0.1 collective-permute-start.18
  22.8 0.5 %collective-permute-start.13 = (f16[376,128]{1,0:T(8,128)(2,1)S(1)}, f16[376,128]{1,0:T(8,128)(2,1)S(1)}, u32[]{:S(2)}, u32[]{:S(2)}) collective-permute-start(f16[376,128]{1,0:T(8,128)(2,1)S(1)} %collective-permute-done.9), channel_id=1, source_target_pairs={{0,1},{1,0},{2,3},{3,2},{4,5},{5,4},{6,7},{7,6},{8,9},{9,8},{10,11... | collective-permute-start | bytes 288776 | tf_op jit(solution)/shard_map/ppermute | solution.py:24
  23.4 2.2 %collective-permute-done.16 = f16[376,128]{1,0:T(8,128)(2,1)S(1)} collective-permute-done((f16[376,128]{1,0:T(8,128)(2,1)S(1)}, f16[376,128]{1,0:T(8,128)(2,1)S(1)}, u32[]{:S(2)}, u32[]{:S(2)}) %collective-permute-start.16) | collective-permute-done | bytes 96288 | tf_op jit(solution)/shard_map/ppermute | solution.py:24
  25.6 0.0 collective-permute-start.10
  25.6 0.1 fusion.11
  25.7 7.1 %collective-permute-done.10 = f16[376,128]{1,0:T(8,128)(2,1)S(1)} collective-permute-done((f16[376,128]{1,0:T(8,128)(2,1)S(1)}, f16[376,128]{1,0:T(8,128)(2,1)S(1)}, u32[]{:S(2)}, u32[]{:S(2)}) %collective-permute-start.10) | collective-permute-done | bytes 96288 | tf_op jit(solution)/shard_map/ppermute | solution.py:24
  32.9 0.0 collective-permute-start.17
  32.9 0.6 %collective-permute-start.11 = (f16[376,128]{1,0:T(8,128)(2,1)S(1)}, f16[376,128]{1,0:T(8,128)(2,1)S(1)}, u32[]{:S(2)}, u32[]{:S(2)}) collective-permute-start(f16[376,128]{1,0:T(8,128)(2,1)S(1)} %collective-permute-done.10), channel_id=1, source_target_pairs={{0,1},{1,0},{2,3},{3,2},{4,5},{5,4},{6,7},{7,6},{8,9},{9,8},{10,11... | collective-permute-start | bytes 288776 | tf_op jit(solution)/shard_map/ppermute | solution.py:24
  33.5 0.6 %collective-permute-done.17 = f16[376,128]{1,0:T(8,128)(2,1)S(1)} collective-permute-done((f16[376,128]{1,0:T(8,128)(2,1)S(1)}, f16[376,128]{1,0:T(8,128)(2,1)S(1)}, u32[]{:S(2)}, u32[]{:S(2)}) %collective-permute-start.17) | collective-permute-done | bytes 96288 | tf_op jit(solution)/shard_map/ppermute | solution.py:24
  34.2 0.2 collective-permute-start.12
  34.4 0.1 fusion.14
  34.5 1.3 %collective-permute-start.4 = (f16[376,256]{1,0:T(8,128)(2,1)S(1)}, f16[376,256]{1,0:T(8,128)(2,1)S(1)}, u32[]{:S(2)}, u32[]{:S(2)}) collective-permute-start(f16[376,256]{1,0:T(8,128)(2,1)S(1)} %collective-permute-done.3), channel_id=1, source_target_pairs={{0,2},{1,3},{2,0},{3,1},{4,6},{5,7},{6,4},{7,5},{8,10},{9,11},{10,... | collective-permute-start | bytes 577544 | tf_op jit(solution)/shard_map/ppermute | solution.py:24
  35.8 0.1 collective-permute-start.15
  35.9 0.0 collective-permute-done.11
  35.9 0.1 fusion.16
  36.0 0.0 collective-permute-done.18
  36.0 0.1 fusion.12
  36.1 2.7 %shard_map.57 = (f32[376,384]{1,0:T(8,128)S(1)}, bf16[256,384]{1,0:T(8,128)(2,1)S(1)}, bf16[256,384]{1,0:T(8,128)(2,1)S(1)}, bf16[128,384]{1,0:T(8,128)(2,1)S(1)...) custom-call(s32[8]{0:T(128)S(1)} %stack.64.refs_0_, ...), custom_call_target="tpu_custom_call" | custom-call | flops 443547648 | bytes 1155072 | tf_op jit(solution)/shard_map/pallas_call | solution.py:121
  38.8 0.0 collective-permute-done.12
  38.9 0.1 fusion.15
  38.9 0.0 collective-permute-done.15
  38.9 0.1 fusion.17
  39.0 3.2 %shard_map.58 = (f32[376,384]{1,0:T(8,128)S(1)}, bf16[256,384]{1,0:T(8,128)(2,1)S(1)}, bf16[128,384]{1,0:T(8,128)(2,1)S(1)}, bf16[256,384]{1,0:T(8,128)(2,1)S(1)}, bf16[128,384]{1,0:T(8,128)(2,1)S(1)}) custom-call(s32[4]{0:T(128)S(1)} %pad_add_fusion.refs_0_, f32[24,384]{1,0:T(8,128)S(1)} %bitcast.36, ...), custom_call_target="tpu_custom_call", output_to_operand_aliasing={{0}: (27, {})} | custom-call | flops 887095296 | bytes 1155072 | tf_op jit(solution)/shard_map/pallas_call | solution.py:121
  42.2 0.5 %collective-permute-start.5 = (f16[376,256]{1,0:T(8,128)(2,1)S(1)}, f16[376,256]{1,0:T(8,128)(2,1)S(1)}, u32[]{:S(2)}, u32[]{:S(2)}) collective-permute-start(f16[376,256]{1,0:T(8,128)(2,1)S(1)} %collective-permute-done.4), channel_id=1, source_target_pairs={{0,1},{1,0},{2,3},{3,2},{4,5},{5,4},{6,7},{7,6},{8,9},{9,8},{10,11... | collective-permute-start | bytes 577544 | tf_op jit(solution)/shard_map/ppermute | solution.py:24
  42.7 0.1 fusion.18
  42.8 0.6 %shard_map.59.refs_6_ = f32[376,384]{1,0:T(8,128)S(1)} custom-call(bf16[376,256]{1,0:T(8,128)(2,1)S(1)} %get-tuple-element.46.refs_0_, bf16[376,256]{1,0:T(8,128)(2,1)S(1)} %get-tuple-element.45.refs_1_, bf16[376,128]{1,0:T(8,128)(2,1)S(1)} %get-tuple-element.58.refs_2_, ...), custom_call_target="tpu_custom_call", output_to_operand_aliasing={{}: (6, {})} | custom-call | flops 221773824 | bytes 1155072 | tf_op jit(solution)/shard_map/pallas_call | solution.py:121
  43.4 0.4 collective-permute-done.5
  43.8 0.1 fusion.13
  43.8 1.4 %shard_map.60 = f32[376,384]{1,0:T(8,128)} custom-call(bf16[376,256]{1,0:T(8,128)(2,1)S(1)} %get-tuple-element.56.refs_0_, bf16[376,256]{1,0:T(8,128)(2,1)S(1)} %get-tuple-element.55.refs_1_, bf16[376,128]{1,0:T(8,128)(2,1)S(1)} %get-tuple-element.68.refs_2_, bf16[376,128]{1,0:T(8,128)(2,1)S(1)} %get-tuple-element.67.refs_3_, ...), custom_call_target="tpu_custom_call" | custom-call | tf_op jit(solution)/shard_map/pallas_call | solution.py:162
  (19 shorter events, 0.2 us)
Async XLA Ops:
  0.0 1.0 %copy-start = (bf16[376,384]{1,0:T(8,128)(2,1)S(1)}, bf16[376,384]{1,0:T(8,128)(2,1)}, u32[]{:S(2)}) copy-start(bf16[376,384]{1,0:T(8,128)(2,1)} %source_ref.1) | copy-start | bytes 866308
  1.0 9.6 %copy-start.2 = (s32[24]{0:T(128)S(1)}, s32[24]{0:T(128)}, u32[]{:S(2)}) copy-start(s32[24]{0:T(128)} %param.7) | copy-start | bytes 292
  1.0 9.7 %copy-start.1 = (s32[6,6]{1,0:T(8,128)S(1)}, s32[6,6]{1,0:T(8,128)}, u32[]{:S(2)}) copy-start(s32[6,6]{1,0:T(8,128)} %param.8) | copy-start | bytes 436
  1.0 11.9 %collective-permute-start.7 = (bf16[376,128]{1,0:T(8,128)(2,1)S(1)}, bf16[376,128]{1,0:T(8,128)(2,1)S(1)}, u32[]{:S(2)}, u32[]{:S(2)}) collective-permute-start(bf16[376,128]{1,0:T(8,128)(2,1)S(1)} %get-tuple-element.24), channel_id=1, source_target_pairs={{0,16},{8,24},{16,0},{24,8},{1,17},{9,25},{17,1},{25,9},{2,18},{10... | collective-permute-start | bytes 288776 | tf_op jit(solution)/shard_map/ppermute | solution.py:206
  4.1 9.2 %collective-permute-start.8 = (bf16[376,128]{1,0:T(8,128)(2,1)S(1)}, bf16[376,128]{1,0:T(8,128)(2,1)S(1)}, u32[]{:S(2)}, u32[]{:S(2)}) collective-permute-start(bf16[376,128]{1,0:T(8,128)(2,1)S(1)} %get-tuple-element.24), channel_id=1, source_target_pairs={{0,24},{8,16},{16,8},{24,0},{1,25},{9,17},{17,9},{25,1},{2,26},{10... | collective-permute-start | bytes 288776 | tf_op jit(solution)/shard_map/ppermute | solution.py:206
  5.5 8.1 %collective-permute-start.6 = (bf16[376,128]{1,0:T(8,128)(2,1)S(1)}, bf16[376,128]{1,0:T(8,128)(2,1)S(1)}, u32[]{:S(2)}, u32[]{:S(2)}) collective-permute-start(bf16[376,128]{1,0:T(8,128)(2,1)S(1)} %get-tuple-element.24), channel_id=1, source_target_pairs={{0,8},{8,0},{16,24},{24,16},{1,9},{9,1},{17,25},{25,17},{2,10},{10... | collective-permute-start | bytes 288776 | tf_op jit(solution)/shard_map/ppermute | solution.py:206
  5.6 12.3 %collective-permute-start.1 = (bf16[376,256]{1,0:T(8,128)(2,1)S(1)}, bf16[376,256]{1,0:T(8,128)(2,1)S(1)}, u32[]{:S(2)}, u32[]{:S(2)}) collective-permute-start(bf16[376,256]{1,0:T(8,128)(2,1)S(1)} %get-tuple-element.23), channel_id=1, source_target_pairs={{0,16},{8,24},{16,0},{24,8},{1,17},{9,25},{17,1},{25,9},{2,18},{10... | collective-permute-start | bytes 577544 | tf_op jit(solution)/shard_map/ppermute | solution.py:206
  7.6 10.6 %collective-permute-start.2 = (bf16[376,256]{1,0:T(8,128)(2,1)S(1)}, bf16[376,256]{1,0:T(8,128)(2,1)S(1)}, u32[]{:S(2)}, u32[]{:S(2)}) collective-permute-start(bf16[376,256]{1,0:T(8,128)(2,1)S(1)} %get-tuple-element.23), channel_id=1, source_target_pairs={{0,24},{8,16},{16,8},{24,0},{1,25},{9,17},{17,9},{25,1},{2,26},{10... | collective-permute-start | bytes 577544 | tf_op jit(solution)/shard_map/ppermute | solution.py:206
  12.9 5.6 %collective-permute-start = (bf16[376,256]{1,0:T(8,128)(2,1)S(1)}, bf16[376,256]{1,0:T(8,128)(2,1)S(1)}, u32[]{:S(2)}, u32[]{:S(2)}) collective-permute-start(bf16[376,256]{1,0:T(8,128)(2,1)S(1)} %get-tuple-element.23), channel_id=1, source_target_pairs={{0,8},{8,0},{16,24},{24,16},{1,9},{9,1},{17,25},{25,17},{2,10},{10... | collective-permute-start | bytes 577544 | tf_op jit(solution)/shard_map/ppermute | solution.py:206
  13.9 9.0 %collective-permute-start.9 = (f16[376,128]{1,0:T(8,128)(2,1)S(1)}, f16[376,128]{1,0:T(8,128)(2,1)S(1)}, u32[]{:S(2)}, u32[]{:S(2)}) collective-permute-start(f16[376,128]{1,0:T(8,128)(2,1)S(1)} %fusion.7), channel_id=1, source_target_pairs={{0,6},{1,7},{2,4},{3,5},{4,2},{5,3},{6,0},{7,1},{8,14},{9,15},{10,... | collective-permute-start | bytes 288776 | tf_op jit(solution)/shard_map/ppermute | solution.py:24
  17.9 7.6 %collective-permute-start.16 = (f16[376,128]{1,0:T(8,128)(2,1)S(1)}, f16[376,128]{1,0:T(8,128)(2,1)S(1)}, u32[]{:S(2)}, u32[]{:S(2)}) collective-permute-start(f16[376,128]{1,0:T(8,128)(2,1)S(1)} %fusion.7), channel_id=1, source_target_pairs={{0,2},{1,3},{2,0},{3,1},{4,6},{5,7},{6,4},{7,5},{8,10},{9,11},{10,... | collective-permute-start | bytes 288776 | tf_op jit(solution)/shard_map/ppermute | solution.py:24
  18.8 15.3 %collective-permute-start.3 = (f16[376,256]{1,0:T(8,128)(2,1)S(1)}, f16[376,256]{1,0:T(8,128)(2,1)S(1)}, u32[]{:S(2)}, u32[]{:S(2)}) collective-permute-start(f16[376,256]{1,0:T(8,128)(2,1)S(1)} %fusion.3), channel_id=1, source_target_pairs={{0,6},{1,7},{2,4},{3,5},{4,2},{5,3},{6,0},{7,1},{8,14},{9,15},{10,... | collective-permute-start | bytes 577544 | tf_op jit(solution)/shard_map/ppermute | solution.py:24
  22.7 13.2 %collective-permute-start.14 = (f16[376,256]{1,0:T(8,128)(2,1)S(1)}, f16[376,256]{1,0:T(8,128)(2,1)S(1)}, u32[]{:S(2)}, u32[]{:S(2)}) collective-permute-start(f16[376,256]{1,0:T(8,128)(2,1)S(1)} %fusion.3), channel_id=1, source_target_pairs={{0,2},{1,3},{2,0},{3,1},{4,6},{5,7},{6,4},{7,5},{8,10},{9,11},{10,... | collective-permute-start | bytes 577544 | tf_op jit(solution)/shard_map/ppermute | solution.py:24
  22.8 13.3 %collective-permute-start.18 = (f16[376,384]{1,0:T(8,128)(2,1)S(1)}, f16[376,384]{1,0:T(8,128)(2,1)S(1)}, u32[]{:S(2)}, u32[]{:S(2)}) collective-permute-start(f16[376,384]{1,0:T(8,128)(2,1)S(1)} %pad_maximum_fusion), channel_id=1, source_target_pairs={{0,1},{1,0},{2,3},{3,2},{4,5},{5,4},{6,7},{7,6},{8,9},{9,8},{10,11... | collective-permute-start | bytes 866312 | tf_op jit(solution)/shard_map/ppermute | solution.py:24
  22.8 10.1 %collective-permute-start.13 = (f16[376,128]{1,0:T(8,128)(2,1)S(1)}, f16[376,128]{1,0:T(8,128)(2,1)S(1)}, u32[]{:S(2)}, u32[]{:S(2)}) collective-permute-start(f16[376,128]{1,0:T(8,128)(2,1)S(1)} %collective-permute-done.9), channel_id=1, source_target_pairs={{0,1},{1,0},{2,3},{3,2},{4,5},{5,4},{6,7},{7,6},{8,9},{9,8},{10,11... | collective-permute-start | bytes 288776 | tf_op jit(solution)/shard_map/ppermute | solution.py:24
  25.6 7.3 %collective-permute-start.10 = (f16[376,128]{1,0:T(8,128)(2,1)S(1)}, f16[376,128]{1,0:T(8,128)(2,1)S(1)}, u32[]{:S(2)}, u32[]{:S(2)}) collective-permute-start(f16[376,128]{1,0:T(8,128)(2,1)S(1)} %collective-permute-done.9), channel_id=1, source_target_pairs={{0,2},{1,3},{2,0},{3,1},{4,6},{5,7},{6,4},{7,5},{8,10},{9,11},{10,... | collective-permute-start | bytes 288776 | tf_op jit(solution)/shard_map/ppermute | solution.py:24
  32.9 1.3 %collective-permute-start.17 = (f16[376,128]{1,0:T(8,128)(2,1)S(1)}, f16[376,128]{1,0:T(8,128)(2,1)S(1)}, u32[]{:S(2)}, u32[]{:S(2)}) collective-permute-start(f16[376,128]{1,0:T(8,128)(2,1)S(1)} %collective-permute-done.16), channel_id=1, source_target_pairs={{0,1},{1,0},{2,3},{3,2},{4,5},{5,4},{6,7},{7,6},{8,9},{9,8},{10,11... | collective-permute-start | bytes 288776 | tf_op jit(solution)/shard_map/ppermute | solution.py:24
  32.9 3.0 %collective-permute-start.11 = (f16[376,128]{1,0:T(8,128)(2,1)S(1)}, f16[376,128]{1,0:T(8,128)(2,1)S(1)}, u32[]{:S(2)}, u32[]{:S(2)}) collective-permute-start(f16[376,128]{1,0:T(8,128)(2,1)S(1)} %collective-permute-done.10), channel_id=1, source_target_pairs={{0,1},{1,0},{2,3},{3,2},{4,5},{5,4},{6,7},{7,6},{8,9},{9,8},{10,11... | collective-permute-start | bytes 288776 | tf_op jit(solution)/shard_map/ppermute | solution.py:24
  34.2 4.6 %collective-permute-start.12 = (f16[376,256]{1,0:T(8,128)(2,1)S(1)}, f16[376,256]{1,0:T(8,128)(2,1)S(1)}, u32[]{:S(2)}, u32[]{:S(2)}) collective-permute-start(f16[376,256]{1,0:T(8,128)(2,1)S(1)} %collective-permute-done.3), channel_id=1, source_target_pairs={{0,1},{1,0},{2,3},{3,2},{4,5},{5,4},{6,7},{7,6},{8,9},{9,8},{10,11... | collective-permute-start | bytes 577544 | tf_op jit(solution)/shard_map/ppermute | solution.py:24
  34.5 7.7 %collective-permute-start.4 = (f16[376,256]{1,0:T(8,128)(2,1)S(1)}, f16[376,256]{1,0:T(8,128)(2,1)S(1)}, u32[]{:S(2)}, u32[]{:S(2)}) collective-permute-start(f16[376,256]{1,0:T(8,128)(2,1)S(1)} %collective-permute-done.3), channel_id=1, source_target_pairs={{0,2},{1,3},{2,0},{3,1},{4,6},{5,7},{6,4},{7,5},{8,10},{9,11},{10,... | collective-permute-start | bytes 577544 | tf_op jit(solution)/shard_map/ppermute | solution.py:24
  35.8 3.1 %collective-permute-start.15 = (f16[376,256]{1,0:T(8,128)(2,1)S(1)}, f16[376,256]{1,0:T(8,128)(2,1)S(1)}, u32[]{:S(2)}, u32[]{:S(2)}) collective-permute-start(f16[376,256]{1,0:T(8,128)(2,1)S(1)} %collective-permute-done.14), channel_id=1, source_target_pairs={{0,1},{1,0},{2,3},{3,2},{4,5},{5,4},{6,7},{7,6},{8,9},{9,8},{10,11... | collective-permute-start | bytes 577544 | tf_op jit(solution)/shard_map/ppermute | solution.py:24
  42.2 1.6 %collective-permute-start.5 = (f16[376,256]{1,0:T(8,128)(2,1)S(1)}, f16[376,256]{1,0:T(8,128)(2,1)S(1)}, u32[]{:S(2)}, u32[]{:S(2)}) collective-permute-start(f16[376,256]{1,0:T(8,128)(2,1)S(1)} %collective-permute-done.4), channel_id=1, source_target_pairs={{0,1},{1,0},{2,3},{3,2},{4,5},{5,4},{6,7},{7,6},{8,9},{9,8},{10,11... | collective-permute-start | bytes 577544 | tf_op jit(solution)/shard_map/ppermute | solution.py:24
